TPU v7x, 32 devices: a whole 2x2x4 slice. The times are simulated.
32 devices in a mesh: seq: 4 (over y, core), shard: 8 (over z, x).
Axes of the slice: x: 2, y: 2, z: 4, core: 2. Of those that a mesh axis runs over, the one named last changes fastest.
Arguments:
- tokens: bfloat16 [16384, 768], P(('shard', 'seq')), may hold values from -6 to 6
- doc_lengths: int32 [32], replicated, may hold values from 1 to 1024, 16384 in all
- joint_weight: bfloat16 [768, 2304], P(('seq', 'shard')), may hold values from -0.21875 to 0.21875
- query_bias: bfloat16 [768], P(('seq', 'shard')), may hold values from -3 to 3
- value_bias: bfloat16 [768], P(('seq', 'shard')), may hold values from -3 to 3
- output_weight: bfloat16 [768, 768], P(('seq', 'shard')), may hold values from -1.75 to 1.75
- output_bias: bfloat16 [768], P(('seq', 'shard')), may hold values from -3 to 3
- first_gain: bfloat16 [768], P(('seq', 'shard')), may hold values from 0.5 to 1.5
- first_shift: bfloat16 [768], P(('seq', 'shard')), may hold values from -3 to 3
- inner_weight: bfloat16 [768, 3072], P(('seq', 'shard')), may hold values from -0.21875 to 0.21875
- inner_bias: bfloat16 [3072], P(('seq', 'shard')), may hold values from -3 to 3
- outer_weight: bfloat16 [3072, 768], P(('seq', 'shard')), may hold values from -0.109375 to 0.109375
- outer_bias: bfloat16 [768], P(('seq', 'shard')), may hold values from -3 to 3
- second_gain: bfloat16 [768], P(('seq', 'shard')), may hold values from 0.5 to 1.5
- second_shift: bfloat16 [768], P(('seq', 'shard')), may hold values from -3 to 3
- cotangent: bfloat16 [16384, 768], P(('shard', 'seq')), may hold values from -6 to 6
Outputs:
- layer_out: bfloat16 [16384, 768], P(('shard', 'seq'))
- tokens_grad: float32 [16384, 768], P(('shard', 'seq'))
- joint_weight_grad: float32 [768, 2304], P(('seq', 'shard'))
- query_bias_grad: float32 [768], P(('seq', 'shard'))
- value_bias_grad: float32 [768], P(('seq', 'shard'))
- output_weight_grad: float32 [768, 768], P(('seq', 'shard'))
- output_bias_grad: float32 [768], P(('seq', 'shard'))
- first_gain_grad: float32 [768], P(('seq', 'shard'))
- first_shift_grad: float32 [768], P(('seq', 'shard'))
- inner_weight_grad: float32 [768, 3072], P(('seq', 'shard'))
- inner_bias_grad: float32 [3072], P(('seq', 'shard'))
- outer_weight_grad: float32 [3072, 768], P(('seq', 'shard'))
- outer_bias_grad: float32 [768], P(('seq', 'shard'))
- second_gain_grad: float32 [768], P(('seq', 'shard'))
- second_shift_grad: float32 [768], P(('seq', 'shard'))
Inputs may be any that keep to these rules, and one draw needn't show every extreme that they name: `doc_lengths`: the documents fill the stream in order; running sums of the lengths before each document are its start offset; the longest has exactly 1024 tokens.
All inputs are finite; a program needn't handle non-finite values.
Results may differ from a plain program's by a relative error of at most 0.013.
The roundings to bfloat16 on the way count: a program that leaves them out, or rounds other values in their place, can miss the bound.
Values may be sent and summed in bfloat16 or wider, within the bound.
No kernel may reach another device: no remote copies, remote signals or barrier semaphores. Data moves between devices by JAX's collectives and lax.ppermute only.
A program may use at most 192 MiB of HBM per device.

v0:
```python
import jax
import jax.numpy as jnp
from jax import lax
from jax.sharding import PartitionSpec as P

D = 768
HEADS = 12
HEAD = 64
DOCMAX = 1024
epsilon = 1e-12


def with_halo(cells, sides, width):
    for axis, dim in sides:
        count = lax.axis_size(axis)
        ends = count - 1
        head = lax.slice_in_dim(cells, 0, width, axis=dim)
        tail = lax.slice_in_dim(cells, cells.shape[dim] - width, cells.shape[dim], axis=dim)
        cells = jnp.concatenate(
            [
                lax.ppermute(tail, axis, [(i, (i + 1) % count) for i in range(ends)]),
                cells,
                lax.ppermute(head, axis, [((i + 1) % count, i) for i in range(ends)]),
            ],
            axis=dim,
        )
    return cells


def normalize_keep(value, gain, shift):
    mean = jnp.mean(value, axis=-1, keepdims=True)
    centred = value - mean
    spread = jnp.mean(centred * centred, axis=-1, keepdims=True)
    scale = lax.rsqrt(spread + epsilon)
    normed = centred * scale
    return (normed * gain + shift, normed, scale)


def normalize_back(grad, normed, scale, gain):
    grad_normed = grad * gain
    first = jnp.mean(grad_normed, axis=-1, keepdims=True)
    second = jnp.mean(grad_normed * normed, axis=-1, keepdims=True)
    result = scale * (grad_normed - first - normed * second)
    return (result, jnp.sum(grad * normed, axis=0), jnp.sum(grad, axis=0))


def doc_ids(doc_lengths, positions, total):
    ends = jnp.cumsum(doc_lengths)
    inside = (ends[None, :] <= positions[:, None]).astype(jnp.int32)
    docs = jnp.sum(inside, axis=1)
    valid = (positions >= 0) & (positions < total)
    return jnp.where(valid, docs, -1)


def activate(value):
    return jax.nn.gelu(value, approximate=True)


def left_product(left, right):
    return jnp.einsum("ta,tb->ab", left, right, preferred_element_type=jnp.float32)


def right_product(left, right):
    return jnp.einsum("tb,ab->ta", left, right, preferred_element_type=jnp.float32)


def body(
    tokens,
    doc_lengths,
    joint_weight,
    query_bias,
    value_bias,
    output_weight,
    output_bias,
    first_gain,
    first_shift,
    inner_weight,
    inner_bias,
    outer_weight,
    outer_bias,
    second_gain,
    second_shift,
    cotangent,
):
    seq_count = lax.axis_size("seq")
    shard_count = lax.axis_size("shard")
    rows = tokens.shape[0]
    groups = HEADS // seq_count
    group_width = groups * HEAD
    block = rows * seq_count
    total = block * shard_count
    span_all = block + 2 * DOCMAX
    query_rows = min(512, block)
    count = block // query_rows
    factor = HEAD ** (-0.5)
    params = (
        joint_weight,
        query_bias,
        value_bias,
        output_weight,
        output_bias,
        first_gain,
        first_shift,
        inner_weight,
        inner_bias,
        outer_weight,
        outer_bias,
        second_gain,
        second_shift,
    )
    full = (
        lax.all_gather(params[0], ("seq", "shard"), axis=0, tiled=True),
        lax.all_gather(params[1], ("seq", "shard"), axis=0, tiled=True),
        lax.all_gather(params[2], ("seq", "shard"), axis=0, tiled=True),
        lax.all_gather(params[3], ("seq", "shard"), axis=0, tiled=True),
        lax.all_gather(params[4], ("seq", "shard"), axis=0, tiled=True),
        lax.all_gather(params[5], ("seq", "shard"), axis=0, tiled=True),
        lax.all_gather(params[6], ("seq", "shard"), axis=0, tiled=True),
        lax.all_gather(params[7], ("seq", "shard"), axis=0, tiled=True),
        lax.all_gather(params[8], ("seq", "shard"), axis=0, tiled=True),
        lax.all_gather(params[9], ("seq", "shard"), axis=0, tiled=True),
        lax.all_gather(params[10], ("seq", "shard"), axis=0, tiled=True),
        lax.all_gather(params[11], ("seq", "shard"), axis=0, tiled=True),
        lax.all_gather(params[12], ("seq", "shard"), axis=0, tiled=True),
    )
    (
        joint_full,
        query_full,
        value_full,
        output_full,
        obias_full,
        gain_one,
        shift_one,
        inner_full,
        ibias_full,
        outer_full,
        ubias_full,
        gain_two,
        shift_two,
    ) = full
    base = lax.axis_index("shard") * block
    query_docs = doc_ids(doc_lengths, base + jnp.arange(block, dtype=jnp.int32), total)
    key_docs = doc_ids(doc_lengths, base - DOCMAX + jnp.arange(span_all, dtype=jnp.int32), total)

    def attend_forward(heads_in):
        queries = heads_in[:, 0].reshape(block, groups, HEAD).transpose(1, 0, 2)
        extended = with_halo(heads_in[:, 1:], (("shard", 0),), DOCMAX)
        ext_keys = extended[:, 0].reshape(span_all, groups, HEAD).transpose(1, 0, 2)
        ext_values = extended[:, 1].reshape(span_all, groups, HEAD).transpose(1, 0, 2)

        def scores_of(index):
            query_start = index * query_rows
            query_blk = lax.dynamic_slice_in_dim(queries, query_start, query_rows, 1)
            mask = (
                lax.dynamic_slice_in_dim(query_docs, query_start, query_rows, 0)[:, None]
                == key_docs[None, :]
            )
            scores = (
                jnp.einsum("gqd,gkd->gqk", query_blk, ext_keys, preferred_element_type=jnp.float32)
                * factor
            )
            return (query_blk, ext_keys, ext_values, mask, scores)

        def forward_block(index):
            query_blk, key_blk, value_blk, mask, scores = scores_of(index)
            scores = jnp.where(mask[None], scores, -jnp.inf)
            top = jnp.max(scores, axis=-1, keepdims=True)
            weights = jnp.exp(scores - top)
            summed = jnp.sum(weights, axis=-1, keepdims=True)
            probs = (weights / summed).astype(jnp.bfloat16)
            context = jnp.einsum(
                "gqk,gkd->gqd", probs, value_blk, preferred_element_type=jnp.float32
            )
            return (context.astype(jnp.bfloat16), top + jnp.log(summed))

        ctx_blocks, lse_blocks = lax.map(forward_block, jnp.arange(count, dtype=jnp.int32))
        context_group = ctx_blocks.transpose(0, 2, 1, 3).reshape(block, group_width)
        return (context_group, lse_blocks, scores_of)

    bias_row = jnp.concatenate([query_full, jnp.zeros_like(query_full), value_full]).astype(
        jnp.float32
    )
    joint = (jnp.dot(tokens, joint_full, preferred_element_type=jnp.float32) + bias_row).astype(
        jnp.bfloat16
    )
    heads_in = lax.all_to_all(
        joint.reshape(rows, 3, seq_count, group_width),
        "seq",
        split_axis=2,
        concat_axis=0,
        tiled=True,
    )
    context_group, lse_blocks, scores_of = attend_forward(heads_in.reshape(block, 3, group_width))
    context = context_group.reshape(seq_count, rows, 1, group_width)
    context_tok = lax.all_to_all(context, "seq", split_axis=0, concat_axis=2, tiled=True).reshape(
        rows, D
    )
    attn = jnp.dot(
        context_tok, output_full, preferred_element_type=jnp.float32
    ) + obias_full.astype(jnp.float32)
    hidden, normed_one, scale_one = normalize_keep(
        tokens.astype(jnp.float32) + attn,
        gain_one.astype(jnp.float32),
        shift_one.astype(jnp.float32),
    )
    hidden_low = hidden.astype(jnp.bfloat16)
    inner = jnp.dot(hidden_low, inner_full, preferred_element_type=jnp.float32) + ibias_full.astype(
        jnp.float32
    )
    active, active_back = jax.vjp(activate, inner)
    active_low = active.astype(jnp.bfloat16)
    outer = jnp.dot(active_low, outer_full, preferred_element_type=jnp.float32) + ubias_full.astype(
        jnp.float32
    )
    result, normed_two, scale_two = normalize_keep(
        hidden + outer, gain_two.astype(jnp.float32), shift_two.astype(jnp.float32)
    )
    layer_out = result.astype(jnp.bfloat16)
    grad_two, grad_gain_two, grad_shift_two = normalize_back(
        cotangent.astype(jnp.float32), normed_two, scale_two, gain_two.astype(jnp.float32)
    )
    grad_outer = grad_two.astype(jnp.bfloat16)
    grad_ubias = jnp.sum(grad_outer.astype(jnp.float32), axis=0)
    grad_outer_weight = left_product(active_low, grad_outer)
    grad_active = right_product(grad_outer, outer_full)
    grad_inner = active_back(grad_active)[0].astype(jnp.bfloat16)
    grad_ibias = jnp.sum(grad_inner.astype(jnp.float32), axis=0)
    grad_inner_weight = left_product(hidden_low, grad_inner)
    grad_hidden = grad_two + right_product(grad_inner, inner_full)
    grad_one, grad_gain_one, grad_shift_one = normalize_back(
        grad_hidden, normed_one, scale_one, gain_one.astype(jnp.float32)
    )
    grad_attn = grad_one.astype(jnp.bfloat16)
    grad_obias = jnp.sum(grad_attn.astype(jnp.float32), axis=0)
    grad_output_weight = left_product(context_tok, grad_attn)
    grad_context = right_product(grad_attn, output_full).astype(jnp.bfloat16)
    grad_group = lax.all_to_all(
        grad_context.reshape(1, rows, seq_count, group_width),
        "seq",
        split_axis=2,
        concat_axis=0,
        tiled=True,
    )
    grad_heads = (
        grad_group.reshape(block, group_width).reshape(block, groups, HEAD).transpose(1, 0, 2)
    )

    def backward_block(carry, inputs):
        index, lse = inputs
        query_blk, key_blk, value_blk, mask, scores = scores_of(index)
        probs = jnp.where(mask[None], jnp.exp(scores - lse), 0.0)
        probs_low = probs.astype(jnp.bfloat16)
        grad_blk = lax.dynamic_slice_in_dim(grad_heads, index * query_rows, query_rows, 1)
        grad_probs = jnp.einsum(
            "gqd,gkd->gqk", grad_blk, value_blk, preferred_element_type=jnp.float32
        )
        weighted = jnp.sum(probs * grad_probs, axis=-1, keepdims=True)
        grad_scores = (probs * (grad_probs - weighted)).astype(jnp.bfloat16)
        grad_query = (
            jnp.einsum("gqk,gkd->gqd", grad_scores, key_blk, preferred_element_type=jnp.float32)
            * factor
        )
        grad_key = (
            jnp.einsum("gqk,gqd->gkd", grad_scores, query_blk, preferred_element_type=jnp.float32)
            * factor
        )
        grad_value = jnp.einsum(
            "gqk,gqd->gkd", probs_low, grad_blk, preferred_element_type=jnp.float32
        )
        current = carry
        carry = current + jnp.stack([grad_key, grad_value])
        return (carry, grad_query)

    start_grads = jnp.zeros((2, groups, span_all, HEAD), jnp.float32)
    grad_keyvals, grad_queries = lax.scan(
        backward_block, start_grads, (jnp.arange(count, dtype=jnp.int32), lse_blocks)
    )
    rims = jnp.concatenate(
        [grad_keyvals[:, :, :DOCMAX], grad_keyvals[:, :, DOCMAX + block :]], axis=2
    )
    received = with_halo(rims.astype(jnp.bfloat16), (("shard", 2),), DOCMAX).astype(rims.dtype)
    from_left = received[:, :, :DOCMAX]
    from_right = received[:, :, 3 * DOCMAX :]
    owned = grad_keyvals[:, :, DOCMAX : DOCMAX + block]
    owned = owned.at[:, :, :DOCMAX].add(from_left)
    owned = owned.at[:, :, block - DOCMAX :].add(from_right)
    grad_queries = grad_queries.transpose(1, 0, 2, 3).reshape(groups, block, HEAD)
    stacked = jnp.concatenate([grad_queries[None], owned], axis=0).astype(jnp.bfloat16)
    stacked = stacked.transpose(2, 0, 1, 3).reshape(block, 3, group_width)
    grad_joint = lax.all_to_all(
        stacked.reshape(block, 3, 1, group_width), "seq", split_axis=0, concat_axis=2, tiled=True
    ).reshape(rows, 3 * D)
    grad_joint_weight = left_product(tokens, grad_joint)
    joint_wide = grad_joint.astype(jnp.float32)
    grad_qbias = jnp.sum(joint_wide[:, :D], axis=0)
    grad_vbias = jnp.sum(joint_wide[:, 2 * D :], axis=0)
    tokens_grad = grad_one + right_product(grad_joint, joint_full)
    terms = (
        grad_joint_weight,
        grad_qbias,
        grad_vbias,
        grad_output_weight,
        grad_obias,
        grad_gain_one,
        grad_shift_one,
        grad_inner_weight,
        grad_ibias,
        grad_outer_weight,
        grad_ubias,
        grad_gain_two,
        grad_shift_two,
    )
    reduced = tuple(
        (
            lax.psum_scatter(terms[0], ("seq", "shard"), scatter_dimension=0, tiled=True),
            lax.psum_scatter(terms[1], ("seq", "shard"), scatter_dimension=0, tiled=True),
            lax.psum_scatter(terms[2], ("seq", "shard"), scatter_dimension=0, tiled=True),
            lax.psum_scatter(terms[3], ("seq", "shard"), scatter_dimension=0, tiled=True),
            lax.psum_scatter(terms[4], ("seq", "shard"), scatter_dimension=0, tiled=True),
            lax.psum_scatter(terms[5], ("seq", "shard"), scatter_dimension=0, tiled=True),
            lax.psum_scatter(terms[6], ("seq", "shard"), scatter_dimension=0, tiled=True),
            lax.psum_scatter(terms[7], ("seq", "shard"), scatter_dimension=0, tiled=True),
            lax.psum_scatter(terms[8], ("seq", "shard"), scatter_dimension=0, tiled=True),
            lax.psum_scatter(terms[9], ("seq", "shard"), scatter_dimension=0, tiled=True),
            lax.psum_scatter(terms[10], ("seq", "shard"), scatter_dimension=0, tiled=True),
            lax.psum_scatter(terms[11], ("seq", "shard"), scatter_dimension=0, tiled=True),
            lax.psum_scatter(terms[12], ("seq", "shard"), scatter_dimension=0, tiled=True),
        )
    )
    return (layer_out, tokens_grad) + tuple(reduced)


def solution(mesh):
    placed = (
        P(("shard", "seq"), None),
        P(),
        P(("seq", "shard"), None),
        P(("seq", "shard")),
        P(("seq", "shard")),
        P(("seq", "shard"), None),
        P(("seq", "shard")),
        P(("seq", "shard")),
        P(("seq", "shard")),
        P(("seq", "shard"), None),
        P(("seq", "shard")),
        P(("seq", "shard"), None),
        P(("seq", "shard")),
        P(("seq", "shard")),
        P(("seq", "shard")),
        P(("shard", "seq"), None),
    )
    return jax.shard_map(
        body,
        mesh=mesh,
        in_specs=placed,
        out_specs=(
            P(("shard", "seq"), None),
            P(("shard", "seq"), None),
            P(("seq", "shard"), None),
            P(("seq", "shard")),
            P(("seq", "shard")),
            P(("seq", "shard"), None),
            P(("seq", "shard")),
            P(("seq", "shard")),
            P(("seq", "shard")),
            P(("seq", "shard"), None),
            P(("seq", "shard")),
            P(("seq", "shard"), None),
            P(("seq", "shard")),
            P(("seq", "shard")),
            P(("seq", "shard")),
        ),
        check_vma=False,
    )
```

profile of v0, /device:TPU:0, one launch (start us, length us, event | category | flops | bytes accessed | tf_op | source)
XLA Modules:
  0.0 1033.4 jit_solution(4330060679045575780)
XLA Ops:
  17.0 42.9 %all-reduce.19 = (bf16[768]{0:T(1024)(128)(2,1)S(1)}, bf16[768]{0:T(1024)(128)(2,1)S(1)}, bf16[768]{0:T(1024)(128)(2,1)}, bf16[768]{0:T(1024)(128)(2,1)}, bf16[7...) all-reduce(bf16[768]{0:T(1024)(128)(2,1)S(1)} %dynamic-update-slice, ...), channel_id=1, replica_groups=mesh['seq'=4,'shard'=8] {'seq','shard'}, use_global_device_ids=true, to_apply=%add.1 | all-reduce | flops 9216 | bytes 36864
  59.9 14.2 %all-gather.5.cloned.1.call-done = bf16[768,2304]{1,0:T(8,128)(2,1)} async-done(((bf16[24,2304]{1,0:T(8,128)(2,1)}), bf16[768,2304]{1,0:T(8,128)(2,1)}) %all-gather.5.cloned.1.call-update) | async-done | bytes 3538960 | tf_op jit(solution)/shard_map/all_gather | solution.py:112
  89.0 28.1 %all-to-all-done = bf16[512,3,4,192]{0,3,1,2:T(8,128)(2,1)S(1)} async-done(((bf16[512,3,4,192]{0,3,1,2:T(8,128)(2,1)}), bf16[512,3,4,192]{0,3,1,2:T(8,128)(2,1)S(1)}, u32[]{:S(2)}, u32[]{:S(2)}) %all-to-all-start) | async-done | bytes 2359328 | tf_op jit(solution)/shard_map/all_to_all | solution.py:186
  130.8 32.3 %collective-permute-done = bf16[1024,2,192]{0,2,1:T(8,128)(2,1)S(1)} collective-permute-done((bf16[1024,2,192]{0,2,1:T(8,128)(2,1)S(1)}, bf16[1024,2,192]{0,2,1:T(8,128)(2,1)S(1)}, u32[]{:S(2)}, u32[]{:S(2)}) %collective-permute-start) | collective-permute-done | bytes 786464 | tf_op jit(solution)/shard_map/ppermute | solution.py:21
  165.5 160.2 %while.27 = (s32[]{:T(128)}, bf16[4,3,512,64]{2,3,1,0:T(8,128)(2,1)}, f32[4,3,512,1]{2,1,3,0:T(4,128)S(1)}, s32[4]{0:T(128)S(1)}, s32[2048]{0:T(1024)S(1)}, /*in...) while((s32[]{:T(128)}, ...), condition=%wide.region_6.7_spmd, body=%wide.region_3.6_spmd.sunk | while | flops 1688304128 | bytes 87503056 | solution.py:176
  168.2 12.2 %fusion.113 = (f32[3,512]{1,0:T(4,128)S(1)}, f32[3,512,4096]{2,1,0:T(8,128)}) fusion(pred[512,4096]{1,0:T(8,128)(4,1)S(1)} %broadcast_compare_fusion.4, bf16[3,4096,64]{1,2,0:T(8,128)(2,1)} %get-tuple-element.530, bf16[3,2048,64]{1,2,0:T(8,128)(2,1)S(1)} %get-tuple-element.529, s32[]{:T(128)S(6)} %select_n.67), kind=kOutput, calls=%fused_computation.3.clone.1 | convolution fusion | flops 824179200 | bytes 29038596 | tf_op jit(solution)/shard_map/while/body/eval_jaxpr/gqd,gkd->gqk/dot_general | solution.py:159
  180.4 12.5 %fusion.114 = f32[3,512]{1,0:T(4,128)S(1)} fusion(f32[3,512,4096]{2,1,0:T(8,128)} %get-tuple-element.482, f32[3,512]{1,0:T(4,128)S(1)} %get-tuple-element.483, pred[512,4096]{1,0:T(8,128)(4,1)S(1)} %broadcast_compare_fusion.4), kind=kLoop, calls=%fused_computation.4.clone.1 | loop fusion | flops 25164288 | bytes 27275264 | tf_op jit(solution)/shard_map/while/body/eval_jaxpr/reduce_sum | solution.py:169
  192.9 13.4 %fusion.115 = bf16[4,3,512,64]{2,3,1,0:T(8,128)(2,1)} fusion(bf16[4,3,512,64]{2,3,1,0:T(8,128)(2,1)} %get-tuple-element.511, s32[]{:T(128)S(6)} %copy.102, bf16[3,4096,64]{1,2,0:T(8,128)(2,1)} %get-tuple-element.531, f32[3,512,4096]{2,1,0:T(8,128)} %get-tuple-element.482, f32[3,512]{1,0:T(4,128)S(1)} %fusion.114, ...), kind=kOutput, calls=%fused_computation.9.clone.1 | convolution fusion | flops 836861952 | bytes 29044740 | tf_op jit(solution)/shard_map/while/body/eval_jaxpr/gqk,gkd->gqd/dot_general | solution.py:171
  208.9 12.2 %fusion.113 = (f32[3,512]{1,0:T(4,128)S(1)}, f32[3,512,4096]{2,1,0:T(8,128)}) fusion(pred[512,4096]{1,0:T(8,128)(4,1)S(1)} %broadcast_compare_fusion.4, bf16[3,4096,64]{1,2,0:T(8,128)(2,1)} %get-tuple-element.530, bf16[3,2048,64]{1,2,0:T(8,128)(2,1)S(1)} %get-tuple-element.529, s32[]{:T(128)S(6)} %select_n.67), kind=kOutput, calls=%fused_computation.3.clone.1 | convolution fusion | flops 824179200 | bytes 29038596 | tf_op jit(solution)/shard_map/while/body/eval_jaxpr/gqd,gkd->gqk/dot_general | solution.py:159
  221.2 11.8 %fusion.114 = f32[3,512]{1,0:T(4,128)S(1)} fusion(f32[3,512,4096]{2,1,0:T(8,128)} %get-tuple-element.482, f32[3,512]{1,0:T(4,128)S(1)} %get-tuple-element.483, pred[512,4096]{1,0:T(8,128)(4,1)S(1)} %broadcast_compare_fusion.4), kind=kLoop, calls=%fused_computation.4.clone.1 | loop fusion | flops 25164288 | bytes 27275264 | tf_op jit(solution)/shard_map/while/body/eval_jaxpr/reduce_sum | solution.py:169
  233.0 13.0 %fusion.115 = bf16[4,3,512,64]{2,3,1,0:T(8,128)(2,1)} fusion(bf16[4,3,512,64]{2,3,1,0:T(8,128)(2,1)} %get-tuple-element.511, s32[]{:T(128)S(6)} %copy.102, bf16[3,4096,64]{1,2,0:T(8,128)(2,1)} %get-tuple-element.531, f32[3,512,4096]{2,1,0:T(8,128)} %get-tuple-element.482, f32[3,512]{1,0:T(4,128)S(1)} %fusion.114, ...), kind=kOutput, calls=%fused_computation.9.clone.1 | convolution fusion | flops 836861952 | bytes 29044740 | tf_op jit(solution)/shard_map/while/body/eval_jaxpr/gqk,gkd->gqd/dot_general | solution.py:171
  248.7 12.3 %fusion.113 = (f32[3,512]{1,0:T(4,128)S(1)}, f32[3,512,4096]{2,1,0:T(8,128)}) fusion(pred[512,4096]{1,0:T(8,128)(4,1)S(1)} %broadcast_compare_fusion.4, bf16[3,4096,64]{1,2,0:T(8,128)(2,1)} %get-tuple-element.530, bf16[3,2048,64]{1,2,0:T(8,128)(2,1)S(1)} %get-tuple-element.529, s32[]{:T(128)S(6)} %select_n.67), kind=kOutput, calls=%fused_computation.3.clone.1 | convolution fusion | flops 824179200 | bytes 29038596 | tf_op jit(solution)/shard_map/while/body/eval_jaxpr/gqd,gkd->gqk/dot_general | solution.py:159
  261.0 11.9 %fusion.114 = f32[3,512]{1,0:T(4,128)S(1)} fusion(f32[3,512,4096]{2,1,0:T(8,128)} %get-tuple-element.482, f32[3,512]{1,0:T(4,128)S(1)} %get-tuple-element.483, pred[512,4096]{1,0:T(8,128)(4,1)S(1)} %broadcast_compare_fusion.4), kind=kLoop, calls=%fused_computation.4.clone.1 | loop fusion | flops 25164288 | bytes 27275264 | tf_op jit(solution)/shard_map/while/body/eval_jaxpr/reduce_sum | solution.py:169
  273.0 13.0 %fusion.115 = bf16[4,3,512,64]{2,3,1,0:T(8,128)(2,1)} fusion(bf16[4,3,512,64]{2,3,1,0:T(8,128)(2,1)} %get-tuple-element.511, s32[]{:T(128)S(6)} %copy.102, bf16[3,4096,64]{1,2,0:T(8,128)(2,1)} %get-tuple-element.531, f32[3,512,4096]{2,1,0:T(8,128)} %get-tuple-element.482, f32[3,512]{1,0:T(4,128)S(1)} %fusion.114, ...), kind=kOutput, calls=%fused_computation.9.clone.1 | convolution fusion | flops 836861952 | bytes 29044740 | tf_op jit(solution)/shard_map/while/body/eval_jaxpr/gqk,gkd->gqd/dot_general | solution.py:171
  288.7 12.2 %fusion.113 = (f32[3,512]{1,0:T(4,128)S(1)}, f32[3,512,4096]{2,1,0:T(8,128)}) fusion(pred[512,4096]{1,0:T(8,128)(4,1)S(1)} %broadcast_compare_fusion.4, bf16[3,4096,64]{1,2,0:T(8,128)(2,1)} %get-tuple-element.530, bf16[3,2048,64]{1,2,0:T(8,128)(2,1)S(1)} %get-tuple-element.529, s32[]{:T(128)S(6)} %select_n.67), kind=kOutput, calls=%fused_computation.3.clone.1 | convolution fusion | flops 824179200 | bytes 29038596 | tf_op jit(solution)/shard_map/while/body/eval_jaxpr/gqd,gkd->gqk/dot_general | solution.py:159
  300.9 11.8 %fusion.114 = f32[3,512]{1,0:T(4,128)S(1)} fusion(f32[3,512,4096]{2,1,0:T(8,128)} %get-tuple-element.482, f32[3,512]{1,0:T(4,128)S(1)} %get-tuple-element.483, pred[512,4096]{1,0:T(8,128)(4,1)S(1)} %broadcast_compare_fusion.4), kind=kLoop, calls=%fused_computation.4.clone.1 | loop fusion | flops 25164288 | bytes 27275264 | tf_op jit(solution)/shard_map/while/body/eval_jaxpr/reduce_sum | solution.py:169
  312.7 13.0 %fusion.115 = bf16[4,3,512,64]{2,3,1,0:T(8,128)(2,1)} fusion(bf16[4,3,512,64]{2,3,1,0:T(8,128)(2,1)} %get-tuple-element.511, s32[]{:T(128)S(6)} %copy.102, bf16[3,4096,64]{1,2,0:T(8,128)(2,1)} %get-tuple-element.531, f32[3,512,4096]{2,1,0:T(8,128)} %get-tuple-element.482, f32[3,512]{1,0:T(4,128)S(1)} %fusion.114, ...), kind=kOutput, calls=%fused_computation.9.clone.1 | convolution fusion | flops 836861952 | bytes 29044740 | tf_op jit(solution)/shard_map/while/body/eval_jaxpr/gqk,gkd->gqd/dot_general | solution.py:171
  329.6 11.2 %all-to-all-done.1 = bf16[4,512,1,192]{1,3,2,0:T(8,128)(2,1)S(1)} async-done(((bf16[4,512,1,192]{1,3,2,0:T(8,128)(2,1)}), bf16[4,512,1,192]{1,3,2,0:T(8,128)(2,1)S(1)}, u32[]{:S(2)}, u32[]{:S(2)}) %all-to-all-start.1) | async-done | bytes 786464 | tf_op jit(solution)/shard_map/all_to_all | solution.py:195
  351.8 7.7 fusion.69
  379.1 10.7 %fusion.54 = f32[3072,768]{1,0:T(8,128)} fusion(f32[512,768]{1,0:T(8,128)} %copy-done.9, f32[512,3072]{1,0:T(8,128)} %fusion.62, f32[3072]{0:T(1024)S(1)} %convert_element_type.104), kind=kOutput, calls=%fused_computation.115 | convolution fusion | flops 2432040960 | bytes 17313792 | tf_op jit(solution)/shard_map/ta,tb->ab/dot_general | solution.py:60
  414.9 362.3 %while.28 = (s32[]{:T(128)}, f32[2,3,4096,64]{2,3,1,0:T(8,128)}, bf16[4,3,512,64]{2,3,1,0:T(8,128)(2,1)}, s32[4]{0:T(128)S(1)}, s32[2048]{0:T(1024)S(1)}, /*inde...) while((s32[]{:T(128)}, f32[2,3,4096,64]{2,3,1,0:T(8,128)}, ...), condition=%wide.region_17.18_spmd.clone, body=%wide.region_15.17_spmd.clone.sunk | while | flops 4128602624 | bytes 284885344 | solution.py:275
  417.7 11.8 %fusion.125 = f32[3,512,4096]{2,1,0:T(8,128)} fusion(bf16[3,4096,64]{1,2,0:T(8,128)(2,1)} %get-tuple-element.573, bf16[3,2048,64]{1,2,0:T(8,128)(2,1)S(1)} %get-tuple-element.572, s32[]{:T(128)S(6)} %select_n.71), kind=kOutput, calls=%fused_computation.34.clone.1 | convolution fusion | flops 805306368 | bytes 26935300 | tf_op jit(solution)/shard_map/while/body/eval_jaxpr/gqd,gkd->gqk/dot_general | solution.py:159
  429.6 12.5 %fusion.126 = f32[1,3,4096,64]{2,3,1,0:T(8,128)} fusion(f32[3,512,4096]{2,1,0:T(8,128)} %fusion.125, f32[3,512]{1,0:T(4,128)S(1)} %dynamic-slice_bitcast_fusion.2, pred[512,4096]{1,0:T(8,128)(4,1)S(1)} %broadcast_compare_fusion.5, bf16[3,2048,64]{1,2,0:T(8,128)(2,1)} %get-tuple-element.575, s32[]{:T(128)S(6)} %select_n.71), kind=kOutput, calls=%fused_computation.23.clone.1 | convolution fusion | flops 830472192 | bytes 30611460 | tf_op jit(solution)/shard_map/while/body/eval_jaxpr/gqk,gqd->gkd/dot_general | solution.py:267
  442.1 18.4 %multiply_reduce_fusion.7 = (f32[3,512]{1,0:T(4,128)S(1)}, f32[3,512,4096]{2,1,0:T(8,128)}) fusion(f32[3,512,4096]{2,1,0:T(8,128)} %fusion.125, f32[3,512]{1,0:T(4,128)S(1)} %dynamic-slice_bitcast_fusion.2, pred[512,4096]{1,0:T(8,128)(4,1)S(1)} %broadcast_compare_fusion.5, bf16[3,4096,64]{1,2,0:T(8,128)(2,1)} %get-tuple-element.576, ...), kind=kOutput, calls=%fused_computation.17.clone.1 | convolution fusion | flops 836762112 | bytes 54210564 | tf_op jit(solution)/shard_map/while/body/eval_jaxpr/gqd,gkd->gqk/dot_general | solution.py:254
  460.4 22.0 %multiply_convert_fusion.5 = bf16[3,512,4096]{2,1,0:T(8,128)(2,1)} fusion(f32[3,512,4096]{2,1,0:T(8,128)} %get-tuple-element.495, f32[3,512,4096]{2,1,0:T(8,128)} %fusion.125, f32[3,512]{1,0:T(4,128)S(1)} %get-tuple-element.496, f32[3,512]{1,0:T(4,128)S(1)} %dynamic-slice_bitcast_fusion.2, pred[512,4096]{1,0:T(8,128)(4,1)S(1)} %broadcast_compare_fusion.5), kind=kLoop, calls=%fused_computation.16.clone.1 | loop fusion | flops 37748736 | bytes 65024000 | tf_op jit(solution)/shard_map/while/body/eval_jaxpr/convert_element_type | solution.py:258
  482.4 9.7 fusion.128
  492.2 7.6 fusion.127
  507.1 12.5 %fusion.125 = f32[3,512,4096]{2,1,0:T(8,128)} fusion(bf16[3,4096,64]{1,2,0:T(8,128)(2,1)} %get-tuple-element.573, bf16[3,2048,64]{1,2,0:T(8,128)(2,1)S(1)} %get-tuple-element.572, s32[]{:T(128)S(6)} %select_n.71), kind=kOutput, calls=%fused_computation.34.clone.1 | convolution fusion | flops 805306368 | bytes 26935300 | tf_op jit(solution)/shard_map/while/body/eval_jaxpr/gqd,gkd->gqk/dot_general | solution.py:159
  519.7 13.2 %fusion.126 = f32[1,3,4096,64]{2,3,1,0:T(8,128)} fusion(f32[3,512,4096]{2,1,0:T(8,128)} %fusion.125, f32[3,512]{1,0:T(4,128)S(1)} %dynamic-slice_bitcast_fusion.2, pred[512,4096]{1,0:T(8,128)(4,1)S(1)} %broadcast_compare_fusion.5, bf16[3,2048,64]{1,2,0:T(8,128)(2,1)} %get-tuple-element.575, s32[]{:T(128)S(6)} %select_n.71), kind=kOutput, calls=%fused_computation.23.clone.1 | convolution fusion | flops 830472192 | bytes 30611460 | tf_op jit(solution)/shard_map/while/body/eval_jaxpr/gqk,gqd->gkd/dot_general | solution.py:267
  532.9 19.1 %multiply_reduce_fusion.7 = (f32[3,512]{1,0:T(4,128)S(1)}, f32[3,512,4096]{2,1,0:T(8,128)}) fusion(f32[3,512,4096]{2,1,0:T(8,128)} %fusion.125, f32[3,512]{1,0:T(4,128)S(1)} %dynamic-slice_bitcast_fusion.2, pred[512,4096]{1,0:T(8,128)(4,1)S(1)} %broadcast_compare_fusion.5, bf16[3,4096,64]{1,2,0:T(8,128)(2,1)} %get-tuple-element.576, ...), kind=kOutput, calls=%fused_computation.17.clone.1 | convolution fusion | flops 836762112 | bytes 54210564 | tf_op jit(solution)/shard_map/while/body/eval_jaxpr/gqd,gkd->gqk/dot_general | solution.py:254
  551.9 22.4 %multiply_convert_fusion.5 = bf16[3,512,4096]{2,1,0:T(8,128)(2,1)} fusion(f32[3,512,4096]{2,1,0:T(8,128)} %get-tuple-element.495, f32[3,512,4096]{2,1,0:T(8,128)} %fusion.125, f32[3,512]{1,0:T(4,128)S(1)} %get-tuple-element.496, f32[3,512]{1,0:T(4,128)S(1)} %dynamic-slice_bitcast_fusion.2, pred[512,4096]{1,0:T(8,128)(4,1)S(1)} %broadcast_compare_fusion.5), kind=kLoop, calls=%fused_computation.16.clone.1 | loop fusion | flops 37748736 | bytes 65024000 | tf_op jit(solution)/shard_map/while/body/eval_jaxpr/convert_element_type | solution.py:258
  574.3 9.7 fusion.128
  598.5 11.7 %fusion.125 = f32[3,512,4096]{2,1,0:T(8,128)} fusion(bf16[3,4096,64]{1,2,0:T(8,128)(2,1)} %get-tuple-element.573, bf16[3,2048,64]{1,2,0:T(8,128)(2,1)S(1)} %get-tuple-element.572, s32[]{:T(128)S(6)} %select_n.71), kind=kOutput, calls=%fused_computation.34.clone.1 | convolution fusion | flops 805306368 | bytes 26935300 | tf_op jit(solution)/shard_map/while/body/eval_jaxpr/gqd,gkd->gqk/dot_general | solution.py:159
  610.2 12.5 %fusion.126 = f32[1,3,4096,64]{2,3,1,0:T(8,128)} fusion(f32[3,512,4096]{2,1,0:T(8,128)} %fusion.125, f32[3,512]{1,0:T(4,128)S(1)} %dynamic-slice_bitcast_fusion.2, pred[512,4096]{1,0:T(8,128)(4,1)S(1)} %broadcast_compare_fusion.5, bf16[3,2048,64]{1,2,0:T(8,128)(2,1)} %get-tuple-element.575, s32[]{:T(128)S(6)} %select_n.71), kind=kOutput, calls=%fused_computation.23.clone.1 | convolution fusion | flops 830472192 | bytes 30611460 | tf_op jit(solution)/shard_map/while/body/eval_jaxpr/gqk,gqd->gkd/dot_general | solution.py:267
  622.7 18.7 %multiply_reduce_fusion.7 = (f32[3,512]{1,0:T(4,128)S(1)}, f32[3,512,4096]{2,1,0:T(8,128)}) fusion(f32[3,512,4096]{2,1,0:T(8,128)} %fusion.125, f32[3,512]{1,0:T(4,128)S(1)} %dynamic-slice_bitcast_fusion.2, pred[512,4096]{1,0:T(8,128)(4,1)S(1)} %broadcast_compare_fusion.5, bf16[3,4096,64]{1,2,0:T(8,128)(2,1)} %get-tuple-element.576, ...), kind=kOutput, calls=%fused_computation.17.clone.1 | convolution fusion | flops 836762112 | bytes 54210564 | tf_op jit(solution)/shard_map/while/body/eval_jaxpr/gqd,gkd->gqk/dot_general | solution.py:254
  641.4 23.7 %multiply_convert_fusion.5 = bf16[3,512,4096]{2,1,0:T(8,128)(2,1)} fusion(f32[3,512,4096]{2,1,0:T(8,128)} %get-tuple-element.495, f32[3,512,4096]{2,1,0:T(8,128)} %fusion.125, f32[3,512]{1,0:T(4,128)S(1)} %get-tuple-element.496, f32[3,512]{1,0:T(4,128)S(1)} %dynamic-slice_bitcast_fusion.2, pred[512,4096]{1,0:T(8,128)(4,1)S(1)} %broadcast_compare_fusion.5), kind=kLoop, calls=%fused_computation.16.clone.1 | loop fusion | flops 37748736 | bytes 65024000 | tf_op jit(solution)/shard_map/while/body/eval_jaxpr/convert_element_type | solution.py:258
  665.1 10.0 fusion.128
  675.1 7.8 fusion.127
  690.3 11.9 %fusion.125 = f32[3,512,4096]{2,1,0:T(8,128)} fusion(bf16[3,4096,64]{1,2,0:T(8,128)(2,1)} %get-tuple-element.573, bf16[3,2048,64]{1,2,0:T(8,128)(2,1)S(1)} %get-tuple-element.572, s32[]{:T(128)S(6)} %select_n.71), kind=kOutput, calls=%fused_computation.34.clone.1 | convolution fusion | flops 805306368 | bytes 26935300 | tf_op jit(solution)/shard_map/while/body/eval_jaxpr/gqd,gkd->gqk/dot_general | solution.py:159
  702.2 12.9 %fusion.126 = f32[1,3,4096,64]{2,3,1,0:T(8,128)} fusion(f32[3,512,4096]{2,1,0:T(8,128)} %fusion.125, f32[3,512]{1,0:T(4,128)S(1)} %dynamic-slice_bitcast_fusion.2, pred[512,4096]{1,0:T(8,128)(4,1)S(1)} %broadcast_compare_fusion.5, bf16[3,2048,64]{1,2,0:T(8,128)(2,1)} %get-tuple-element.575, s32[]{:T(128)S(6)} %select_n.71), kind=kOutput, calls=%fused_computation.23.clone.1 | convolution fusion | flops 830472192 | bytes 30611460 | tf_op jit(solution)/shard_map/while/body/eval_jaxpr/gqk,gqd->gkd/dot_general | solution.py:267
  715.0 18.3 %multiply_reduce_fusion.7 = (f32[3,512]{1,0:T(4,128)S(1)}, f32[3,512,4096]{2,1,0:T(8,128)}) fusion(f32[3,512,4096]{2,1,0:T(8,128)} %fusion.125, f32[3,512]{1,0:T(4,128)S(1)} %dynamic-slice_bitcast_fusion.2, pred[512,4096]{1,0:T(8,128)(4,1)S(1)} %broadcast_compare_fusion.5, bf16[3,4096,64]{1,2,0:T(8,128)(2,1)} %get-tuple-element.576, ...), kind=kOutput, calls=%fused_computation.17.clone.1 | convolution fusion | flops 836762112 | bytes 54210564 | tf_op jit(solution)/shard_map/while/body/eval_jaxpr/gqd,gkd->gqk/dot_general | solution.py:254
  733.3 22.2 %multiply_convert_fusion.5 = bf16[3,512,4096]{2,1,0:T(8,128)(2,1)} fusion(f32[3,512,4096]{2,1,0:T(8,128)} %get-tuple-element.495, f32[3,512,4096]{2,1,0:T(8,128)} %fusion.125, f32[3,512]{1,0:T(4,128)S(1)} %get-tuple-element.496, f32[3,512]{1,0:T(4,128)S(1)} %dynamic-slice_bitcast_fusion.2, pred[512,4096]{1,0:T(8,128)(4,1)S(1)} %broadcast_compare_fusion.5), kind=kLoop, calls=%fused_computation.16.clone.1 | loop fusion | flops 37748736 | bytes 65024000 | tf_op jit(solution)/shard_map/while/body/eval_jaxpr/convert_element_type | solution.py:258
  755.5 9.8 fusion.128
  792.9 27.0 %collective-permute-done.2 = bf16[2,3,1024,64]{2,3,1,0:T(8,128)(2,1)} collective-permute-done((bf16[2,3,1024,64]{2,3,1,0:T(8,128)(2,1)}, bf16[2,3,1024,64]{2,3,1,0:T(8,128)(2,1)}, u32[]{:S(2)}, u32[]{:S(2)}) %collective-permute-start.2) | collective-permute-done | bytes 786464 | tf_op jit(solution)/shard_map/ppermute | solution.py:21
  829.3 53.8 %all_to_all.60 = bf16[2048,3,1,192]{3,1,2,0:T(4,128)(2,1)} all-to-all(bf16[2048,3,1,192]{3,1,2,0:T(4,128)(2,1)} %copy.80), channel_id=1, replica_groups=mesh['seq'=4,'shard'=8] {'seq'}, dimensions={0} | all-to-all | bytes 4718592 | tf_op jit(solution)/shard_map/all_to_all | solution.py:290
  897.8 8.0 copy.85
  907.3 42.3 %all-reduce.18 = (f32[768]{0:T(1024)S(1)}, f32[768]{0:T(1024)S(1)}, f32[768]{0:T(1024)S(1)}, f32[768]{0:T(1024)S(1)}, f32[768]{0:T(1024)S(1)}, /*index=5*/f32[30...) all-reduce(f32[768]{0:T(1024)S(1)} %get-tuple-element.276, ...), channel_id=3, replica_groups=mesh['seq'=4,'shard'=8] {'seq','shard'}, use_global_device_ids=true, to_apply=%region_20.21.clone | all-reduce | flops 9216 | bytes 73728
  960.5 65.6 %reduce-scatter.13.cloned.1.call-done = f32[24,2304]{1,0:T(8,128)} async-done(((f32[768,2304]{1,0:T(8,128)}), f32[24,2304]{1,0:T(8,128)}) %reduce-scatter.13.cloned.1.call-update) | async-done | bytes 221200
  (267 shorter events, 200.3 us)
Async XLA Ops:
  7.2 66.9 %all-gather.5.cloned.1.call-start = ((), (), s32[]{:S(2)}) async-start(), calls=%async_computation.8 | async-start | bytes 3649536 | tf_op jit(solution)/shard_map/all_gather | solution.py:112
  7.9 321.7 %all-gather.7.cloned.1.call-start = ((), (), s32[]{:S(2)}) async-start(), calls=%async_computation.9 | async-start | bytes 1216512 | tf_op jit(solution)/shard_map/all_gather | solution.py:115
  8.7 336.1 %all-gather.9.cloned.1.call-start = ((), (), s32[]{:S(2)}) async-start(), calls=%async_computation.10 | async-start | bytes 4866048 | tf_op jit(solution)/shard_map/all_gather | solution.py:119
  84.3 4.4 copy-start.26
  84.3 32.8 %all-to-all-start = ((bf16[512,3,4,192]{0,3,1,2:T(8,128)(2,1)}), bf16[512,3,4,192]{0,3,1,2:T(8,128)(2,1)S(1)}, u32[]{:S(2)}, u32[]{:S(2)}) async-start(bf16[512,3,4,192]{0,3,1,2:T(8,128)(2,1)} %copy.74), calls=%async_computation | async-start | bytes 4718592 | tf_op jit(solution)/shard_map/all_to_all | solution.py:186
  88.1 263.7 %all-gather.11.cloned.1.call-start = ((), (), s32[]{:S(2)}) async-start(), calls=%async_computation.11 | async-start | bytes 4866048 | tf_op jit(solution)/shard_map/all_gather | solution.py:121
  125.1 5.7 copy-start.3
  125.3 37.9 %collective-permute-start = (bf16[1024,2,192]{0,2,1:T(8,128)(2,1)S(1)}, bf16[1024,2,192]{0,2,1:T(8,128)(2,1)S(1)}, u32[]{:S(2)}, u32[]{:S(2)}) collective-permute-start(bf16[1024,2,192]{0,2,1:T(8,128)(2,1)S(1)} %get-tuple-element.355), channel_id=1, source_target_pairs={{0,1},{1,2},{2,3},{3,4},{4,5},{5,6},{6,7},{8,9},{9,10},{10,11},{11... | collective-permute-start | bytes 2359304 | tf_op jit(solution)/shard_map/ppermute | solution.py:21
  128.7 34.5 %collective-permute-start.1 = (bf16[1024,2,192]{0,2,1:T(8,128)(2,1)S(1)}, bf16[1024,2,192]{0,2,1:T(8,128)(2,1)S(1)}, u32[]{:S(2)}, u32[]{:S(2)}) collective-permute-start(bf16[1024,2,192]{0,2,1:T(8,128)(2,1)S(1)} %get-tuple-element.356), channel_id=1, source_target_pairs={{1,0},{2,1},{3,2},{4,3},{5,4},{6,5},{7,6},{9,8},{10,9},{11,10},{12... | collective-permute-start | bytes 2359304 | tf_op jit(solution)/shard_map/ppermute | solution.py:23
  165.5 164.0 %copy-start.25 = (bf16[768]{0:T(1024)(128)(2,1)S(1)}, bf16[768]{0:T(1024)(128)(2,1)}, u32[]{:S(2)}) copy-start(bf16[768]{0:T(1024)(128)(2,1)} %get-tuple-element.339) | copy-start | bytes 4612
  165.5 164.0 %copy-start.24 = (bf16[768]{0:T(1024)(128)(2,1)S(1)}, bf16[768]{0:T(1024)(128)(2,1)}, u32[]{:S(2)}) copy-start(bf16[768]{0:T(1024)(128)(2,1)} %get-tuple-element.338) | copy-start | bytes 4612
  165.5 164.0 %copy-start.23 = (bf16[768]{0:T(1024)(128)(2,1)S(1)}, bf16[768]{0:T(1024)(128)(2,1)}, u32[]{:S(2)}) copy-start(bf16[768]{0:T(1024)(128)(2,1)} %get-tuple-element.342) | copy-start | bytes 4612
  165.5 164.0 %copy-start.22 = (bf16[768]{0:T(1024)(128)(2,1)S(1)}, bf16[768]{0:T(1024)(128)(2,1)}, u32[]{:S(2)}) copy-start(bf16[768]{0:T(1024)(128)(2,1)} %get-tuple-element.336) | copy-start | bytes 4612
  165.5 164.1 %copy-start.21 = (bf16[768]{0:T(1024)(128)(2,1)S(1)}, bf16[768]{0:T(1024)(128)(2,1)}, u32[]{:S(2)}) copy-start(bf16[768]{0:T(1024)(128)(2,1)} %get-tuple-element.337) | copy-start | bytes 4612
  165.5 164.1 %copy-start.20 = (bf16[768]{0:T(1024)(128)(2,1)S(1)}, bf16[768]{0:T(1024)(128)(2,1)}, u32[]{:S(2)}) copy-start(bf16[768]{0:T(1024)(128)(2,1)} %get-tuple-element.341) | copy-start | bytes 4612
  165.5 164.1 %copy-start.17 = (bf16[3072]{0:T(1024)(128)(2,1)S(1)}, bf16[3072]{0:T(1024)(128)(2,1)}, u32[]{:S(2)}) copy-start(bf16[3072]{0:T(1024)(128)(2,1)} %get-tuple-element.340) | copy-start | bytes 18436
  325.7 15.1 %all-to-all-start.1 = ((bf16[4,512,1,192]{1,3,2,0:T(8,128)(2,1)}), bf16[4,512,1,192]{1,3,2,0:T(8,128)(2,1)S(1)}, u32[]{:S(2)}, u32[]{:S(2)}) async-start(bf16[4,512,1,192]{1,3,2,0:T(8,128)(2,1)} %bitcast.14), calls=%async_computation.1 | async-start | bytes 1572864 | tf_op jit(solution)/shard_map/all_to_all | solution.py:195
  329.2 631.2 %reduce-scatter.7.cloned.1.call-start = ((), (), s32[]{:S(2)}) async-start(), calls=%async_computation.12 | async-start | bytes 2433024 | tf_op jit(solution)/shard_map/reduce_scatter | solution.py:318
  351.8 8.1 copy-start.8
  351.8 11.6 %copy-start.28 = (f32[512,3072]{1,0:T(8,128)S(1)}, f32[512,3072]{1,0:T(8,128)}, u32[]{:S(2)}) copy-start(f32[512,3072]{1,0:T(8,128)} %fusion.62) | copy-start | bytes 18874372
  359.9 3.5 copy-start.27
  361.2 9.3 slice-start.3
  363.4 7.1 copy-start.9
  363.4 7.1 slice-start.4
  370.5 3.6 copy-start.29
  378.7 581.8 %reduce-scatter.11.cloned.1.call-start = ((), (), s32[]{:S(2)}) async-start(), calls=%async_computation.14 | async-start | bytes 9732096 | tf_op jit(solution)/shard_map/reduce_scatter | solution.py:324
  395.8 15.9 %all-to-all-start.2 = ((bf16[1,512,4,192]{1,3,0,2:T(8,128)(2,1)}), bf16[1,512,4,192]{1,3,0,2:T(8,128)(2,1)}, u32[]{:S(2)}, u32[]{:S(2)}) async-start(bf16[1,512,4,192]{1,3,0,2:T(8,128)(2,1)} %bitcast.132), calls=%async_computation.2 | async-start | bytes 1572864 | tf_op jit(solution)/shard_map/all_to_all | solution.py:237
  400.0 560.5 %reduce-scatter.9.cloned.1.call-start = ((), (), s32[]{:S(2)}) async-start(), calls=%async_computation.13 | async-start | bytes 9732096 | tf_op jit(solution)/shard_map/reduce_scatter | solution.py:322
  407.4 618.8 %reduce-scatter.13.cloned.1.call-start = ((), (), s32[]{:S(2)}) async-start(), calls=%async_computation.15 | async-start | bytes 7299072
  482.4 17.3 %slice-start = ((s8[6291456]{0:T(1024)(128)(4,1)}), s8[2097152]{0:T(1024)(128)(4,1)S(1)}, s32[]{:S(2)}) async-start(s8[6291456]{0:T(1024)(128)(4,1)} %bitcast.118), calls=%async_computation.16 | async-start | bytes 4194304 | tf_op jit(solution)/shard_map/while
  492.2 7.6 slice-start.1
  492.2 7.6 copy-start.2
  501.8 2.6 copy-start
  574.3 16.8 %slice-start = ((s8[6291456]{0:T(1024)(128)(4,1)}), s8[2097152]{0:T(1024)(128)(4,1)S(1)}, s32[]{:S(2)}) async-start(s8[6291456]{0:T(1024)(128)(4,1)} %bitcast.118), calls=%async_computation.16 | async-start | bytes 4194304 | tf_op jit(solution)/shard_map/while
  584.1 7.1 slice-start.1
  584.1 7.1 copy-start.2
  593.2 2.6 copy-start
  665.1 17.9 %slice-start = ((s8[6291456]{0:T(1024)(128)(4,1)}), s8[2097152]{0:T(1024)(128)(4,1)S(1)}, s32[]{:S(2)}) async-start(s8[6291456]{0:T(1024)(128)(4,1)} %bitcast.118), calls=%async_computation.16 | async-start | bytes 4194304 | tf_op jit(solution)/shard_map/while
  675.1 7.9 slice-start.1
  675.1 7.9 copy-start.2
  685.0 2.6 copy-start
  755.5 16.9 %slice-start = ((s8[6291456]{0:T(1024)(128)(4,1)}), s8[2097152]{0:T(1024)(128)(4,1)S(1)}, s32[]{:S(2)}) async-start(s8[6291456]{0:T(1024)(128)(4,1)} %bitcast.118), calls=%async_computation.16 | async-start | bytes 4194304 | tf_op jit(solution)/shard_map/while
  765.4 7.0 slice-start.1
  765.4 7.1 copy-start.2
  774.5 2.6 copy-start
  777.3 11.0 %copy-start.1 = (f32[2,3,4096,64]{2,3,1,0:T(8,128)S(1)}, f32[2,3,4096,64]{2,3,1,0:T(8,128)}, u32[]{:S(2)}) copy-start(f32[2,3,4096,64]{2,3,1,0:T(8,128)} %get-tuple-element.148) | copy-start | bytes 18874372
  782.0 37.8 %collective-permute-start.2 = (bf16[2,3,1024,64]{2,3,1,0:T(8,128)(2,1)}, bf16[2,3,1024,64]{2,3,1,0:T(8,128)(2,1)}, u32[]{:S(2)}, u32[]{:S(2)}) collective-permute-start(bf16[2,3,1024,64]{2,3,1,0:T(8,128)(2,1)} %get-tuple-element.351), channel_id=1, source_target_pairs={{0,1},{1,2},{2,3},{3,4},{4,5},{5,6},{6,7},{8,9},{9,10},{10,11},{11... | collective-permute-start | bytes 2359304 | tf_op jit(solution)/shard_map/ppermute | solution.py:21
  786.8 33.0 %collective-permute-start.3 = (bf16[2,3,1024,64]{2,3,1,0:T(8,128)(2,1)}, bf16[2,3,1024,64]{2,3,1,0:T(8,128)(2,1)}, u32[]{:S(2)}, u32[]{:S(2)}) collective-permute-start(bf16[2,3,1024,64]{2,3,1,0:T(8,128)(2,1)} %get-tuple-element.352), channel_id=1, source_target_pairs={{1,0},{2,1},{3,2},{4,3},{5,4},{6,5},{7,6},{9,8},{10,9},{11,10},{12... | collective-permute-start | bytes 2359304 | tf_op jit(solution)/shard_map/ppermute | solution.py:23
  (14 other events, 16.2 us)
Sparse Core Ops, SparseCore 0:
  11.0 63.0 all-gather.4
  77.1 53.0 all-gather.6
  133.2 68.0 all-gather.8
  204.0 62.5 all-gather.10
  378.8 98.7 reduce-scatter.6
  484.9 134.7 reduce-scatter.10
  626.2 134.5 reduce-scatter.8
  906.0 120.0 reduce-scatter.12
where the time goes:
time: 1040 us; the launch traced here: 1030 us
  matrix products  412 us (40%)
  waiting for transfers between devices  185 us (18%)
  other arithmetic  171 us (16%)
  blocking collectives  139 us (13%)
  local copies, waits for them, and re-layouts  81 us (8%)
  starting transfers between devices  23.8 us (2%)
  between operations  15.2 us (1%)
    dot_general x8, matrix products, scores_of(): jnp.einsum('gqd,gkd->gqk', query_blk, ext_keys, preferred_element_type=jn...  96.9 us
    convert_element_type x4, other arithmetic, backward_block(): grad_scores = (probs * (grad_probs - weighted)).astype(jnp.bfloat16)  90.3 us
    unnamed x2, blocking collectives  85.2 us
    dot_general x4, matrix products, backward_block(): jnp.einsum('gqd,gkd->gqk', grad_blk, value_blk, preferred_element_type=jn...  74.4 us
    unnamed x9, waiting for transfers between devices  68.3 us
    ppermute x2, waiting for transfers between devices, with_halo(): lax.ppermute(tail, axis, [(i, (i + 1) % count) for i in range(ends)])  59.3 us
    all_to_all x1, blocking collectives, body(): lax.all_to_all(stacked.reshape(block, 3, 1, group_width), 'seq', split_ax...  53.8 us
    dot_general x4, matrix products, forward_block(): jnp.einsum('gqk,gkd->gqd', probs, value_blk, preferred_element_type=jnp.f...  52.5 us
  transfers between devices with their start and end apart: 15, of which 7 were waited for; matrix products, arithmetic and copies ran while one was open for 60% of the time, Pallas kernels for 0%

commit v1 on v0

--- a/solution.py
+++ b/solution.py
@@ -287,9 +287,19 @@
     grad_queries = grad_queries.transpose(1, 0, 2, 3).reshape(groups, block, HEAD)
     stacked = jnp.concatenate([grad_queries[None], owned], axis=0).astype(jnp.bfloat16)
     stacked = stacked.transpose(2, 0, 1, 3).reshape(block, 3, group_width)
-    grad_joint = lax.all_to_all(
-        stacked.reshape(block, 3, 1, group_width), "seq", split_axis=0, concat_axis=2, tiled=True
-    ).reshape(rows, 3 * D)
+
+    def do_shapes_on(local_block, across):
+        return jnp.concatenate(
+            lax.all_to_all(
+                jnp.stack(jnp.split(local_block, lax.axis_size(across), axis=0), axis=0),
+                across,
+                0,
+                0,
+            ),
+            axis=2,
+        )
+
+    grad_joint = do_shapes_on(stacked.reshape(block, 3, 1, group_width), "seq").reshape(rows, 3 * D)
     grad_joint_weight = left_product(tokens, grad_joint)
     joint_wide = grad_joint.astype(jnp.float32)
     grad_qbias = jnp.sum(joint_wide[:, :D], axis=0)

time: 1040 us -> 1010 us (0.971)
  blocking collectives: 139 us -> 116 us
  local copies, waits for them, and re-layouts: 81 us -> 68 us
    all_to_all x1, blocking collectives: 53.8 us -> 31 us  [do_shapes_on(): lax.all_to_all(jnp.stack(jnp.split(local_block, lax.axis_size(across), ax...]
  transfers between devices with their start and end apart: 15 -> 15, of which waited for: 7 -> 7; matrix products, arithmetic and copies ran while one was open for 60% -> 61% of each run, Pallas kernels for 0% -> 0%
where the time goes in v1:
time: 1010 us; the launch traced here: 997 us
  matrix products  412 us (41%)
  waiting for transfers between devices  185 us (18%)
  other arithmetic  171 us (17%)
  blocking collectives  116 us (11%)
  local copies, waits for them, and re-layouts  68 us (7%)
  starting transfers between devices  23.6 us (2%)
  between operations  15 us (1%)
    dot_general x8, matrix products, scores_of(): jnp.einsum('gqd,gkd->gqk', query_blk, ext_keys, preferred_element_type=jn...  96.9 us
    convert_element_type x4, other arithmetic, backward_block(): grad_scores = (probs * (grad_probs - weighted)).astype(jnp.bfloat16)  90.4 us
    unnamed x2, blocking collectives  85.1 us
    dot_general x4, matrix products, backward_block(): jnp.einsum('gqd,gkd->gqk', grad_blk, value_blk, preferred_element_type=jn...  74.3 us
    unnamed x9, waiting for transfers between devices  68.4 us
    ppermute x2, waiting for transfers between devices, with_halo(): lax.ppermute(tail, axis, [(i, (i + 1) % count) for i in range(ends)])  59.5 us
    dot_general x4, matrix products, forward_block(): jnp.einsum('gqk,gkd->gqd', probs, value_blk, preferred_element_type=jnp.f...  52.5 us
    dot_general x4, matrix products, backward_block(): jnp.einsum('gqk,gqd->gkd', probs_low, grad_blk, preferred_element_type=jn...  50.8 us
  transfers between devices with their start and end apart: 15, of which 7 were waited for; matrix products, arithmetic and copies ran while one was open for 61% of the time, Pallas kernels for 0%

profile of v1, /device:TPU:0, one launch (start us, length us, event | category | flops | bytes accessed | tf_op | source)
XLA Modules:
  0.0 997.3 jit_solution(5803356542878531766)
XLA Ops:
  17.0 42.9 %all-reduce.19 = (bf16[768]{0:T(1024)(128)(2,1)S(1)}, bf16[768]{0:T(1024)(128)(2,1)S(1)}, bf16[768]{0:T(1024)(128)(2,1)}, bf16[768]{0:T(1024)(128)(2,1)}, bf16[7...) all-reduce(bf16[768]{0:T(1024)(128)(2,1)S(1)} %dynamic-update-slice, ...), channel_id=1, replica_groups=mesh['seq'=4,'shard'=8] {'seq','shard'}, use_global_device_ids=true, to_apply=%add.1 | all-reduce | flops 9216 | bytes 36864
  59.9 14.2 %all-gather.5.cloned.1.call-done = bf16[768,2304]{1,0:T(8,128)(2,1)} async-done(((bf16[24,2304]{1,0:T(8,128)(2,1)}), bf16[768,2304]{1,0:T(8,128)(2,1)}) %all-gather.5.cloned.1.call-update) | async-done | bytes 3538960 | tf_op jit(solution)/shard_map/all_gather | solution.py:112
  89.0 28.1 %all-to-all-done = bf16[512,3,4,192]{0,3,1,2:T(8,128)(2,1)S(1)} async-done(((bf16[512,3,4,192]{0,3,1,2:T(8,128)(2,1)}), bf16[512,3,4,192]{0,3,1,2:T(8,128)(2,1)S(1)}, u32[]{:S(2)}, u32[]{:S(2)}) %all-to-all-start) | async-done | bytes 2359328 | tf_op jit(solution)/shard_map/all_to_all | solution.py:186
  130.7 32.6 %collective-permute-done = bf16[1024,2,192]{0,2,1:T(8,128)(2,1)S(1)} collective-permute-done((bf16[1024,2,192]{0,2,1:T(8,128)(2,1)S(1)}, bf16[1024,2,192]{0,2,1:T(8,128)(2,1)S(1)}, u32[]{:S(2)}, u32[]{:S(2)}) %collective-permute-start) | collective-permute-done | bytes 786464 | tf_op jit(solution)/shard_map/ppermute | solution.py:21
  165.6 160.2 %while.27 = (s32[]{:T(128)}, bf16[4,3,512,64]{2,3,1,0:T(8,128)(2,1)}, f32[4,3,512,1]{2,1,3,0:T(4,128)S(1)}, s32[4]{0:T(128)S(1)}, s32[2048]{0:T(1024)S(1)}, /*in...) while((s32[]{:T(128)}, ...), condition=%wide.region_6.7_spmd, body=%wide.region_3.6_spmd.sunk | while | flops 1688304128 | bytes 87503056 | solution.py:176
  168.2 12.2 %fusion.114 = (f32[3,512]{1,0:T(4,128)S(1)}, f32[3,512,4096]{2,1,0:T(8,128)}) fusion(pred[512,4096]{1,0:T(8,128)(4,1)S(1)} %broadcast_compare_fusion.4, bf16[3,4096,64]{1,2,0:T(8,128)(2,1)} %get-tuple-element.519, bf16[3,2048,64]{1,2,0:T(8,128)(2,1)S(1)} %get-tuple-element.518, s32[]{:T(128)S(6)} %select_n.67), kind=kOutput, calls=%fused_computation.3.clone.1 | convolution fusion | flops 824179200 | bytes 29038596 | tf_op jit(solution)/shard_map/while/body/eval_jaxpr/gqd,gkd->gqk/dot_general | solution.py:159
  180.4 12.5 %fusion.115 = f32[3,512]{1,0:T(4,128)S(1)} fusion(f32[3,512,4096]{2,1,0:T(8,128)} %get-tuple-element.471, f32[3,512]{1,0:T(4,128)S(1)} %get-tuple-element.472, pred[512,4096]{1,0:T(8,128)(4,1)S(1)} %broadcast_compare_fusion.4), kind=kLoop, calls=%fused_computation.4.clone.1 | loop fusion | flops 25164288 | bytes 27275264 | tf_op jit(solution)/shard_map/while/body/eval_jaxpr/reduce_sum | solution.py:169
  192.9 13.4 %fusion.116 = bf16[4,3,512,64]{2,3,1,0:T(8,128)(2,1)} fusion(bf16[4,3,512,64]{2,3,1,0:T(8,128)(2,1)} %get-tuple-element.500, s32[]{:T(128)S(6)} %copy.84, bf16[3,4096,64]{1,2,0:T(8,128)(2,1)} %get-tuple-element.520, f32[3,512,4096]{2,1,0:T(8,128)} %get-tuple-element.471, f32[3,512]{1,0:T(4,128)S(1)} %fusion.115, ...), kind=kOutput, calls=%fused_computation.9.clone.1 | convolution fusion | flops 836861952 | bytes 29044740 | tf_op jit(solution)/shard_map/while/body/eval_jaxpr/gqk,gkd->gqd/dot_general | solution.py:171
  209.0 12.2 %fusion.114 = (f32[3,512]{1,0:T(4,128)S(1)}, f32[3,512,4096]{2,1,0:T(8,128)}) fusion(pred[512,4096]{1,0:T(8,128)(4,1)S(1)} %broadcast_compare_fusion.4, bf16[3,4096,64]{1,2,0:T(8,128)(2,1)} %get-tuple-element.519, bf16[3,2048,64]{1,2,0:T(8,128)(2,1)S(1)} %get-tuple-element.518, s32[]{:T(128)S(6)} %select_n.67), kind=kOutput, calls=%fused_computation.3.clone.1 | convolution fusion | flops 824179200 | bytes 29038596 | tf_op jit(solution)/shard_map/while/body/eval_jaxpr/gqd,gkd->gqk/dot_general | solution.py:159
  221.2 11.8 %fusion.115 = f32[3,512]{1,0:T(4,128)S(1)} fusion(f32[3,512,4096]{2,1,0:T(8,128)} %get-tuple-element.471, f32[3,512]{1,0:T(4,128)S(1)} %get-tuple-element.472, pred[512,4096]{1,0:T(8,128)(4,1)S(1)} %broadcast_compare_fusion.4), kind=kLoop, calls=%fused_computation.4.clone.1 | loop fusion | flops 25164288 | bytes 27275264 | tf_op jit(solution)/shard_map/while/body/eval_jaxpr/reduce_sum | solution.py:169
  233.0 13.1 %fusion.116 = bf16[4,3,512,64]{2,3,1,0:T(8,128)(2,1)} fusion(bf16[4,3,512,64]{2,3,1,0:T(8,128)(2,1)} %get-tuple-element.500, s32[]{:T(128)S(6)} %copy.84, bf16[3,4096,64]{1,2,0:T(8,128)(2,1)} %get-tuple-element.520, f32[3,512,4096]{2,1,0:T(8,128)} %get-tuple-element.471, f32[3,512]{1,0:T(4,128)S(1)} %fusion.115, ...), kind=kOutput, calls=%fused_computation.9.clone.1 | convolution fusion | flops 836861952 | bytes 29044740 | tf_op jit(solution)/shard_map/while/body/eval_jaxpr/gqk,gkd->gqd/dot_general | solution.py:171
  248.7 12.3 %fusion.114 = (f32[3,512]{1,0:T(4,128)S(1)}, f32[3,512,4096]{2,1,0:T(8,128)}) fusion(pred[512,4096]{1,0:T(8,128)(4,1)S(1)} %broadcast_compare_fusion.4, bf16[3,4096,64]{1,2,0:T(8,128)(2,1)} %get-tuple-element.519, bf16[3,2048,64]{1,2,0:T(8,128)(2,1)S(1)} %get-tuple-element.518, s32[]{:T(128)S(6)} %select_n.67), kind=kOutput, calls=%fused_computation.3.clone.1 | convolution fusion | flops 824179200 | bytes 29038596 | tf_op jit(solution)/shard_map/while/body/eval_jaxpr/gqd,gkd->gqk/dot_general | solution.py:159
  261.1 11.9 %fusion.115 = f32[3,512]{1,0:T(4,128)S(1)} fusion(f32[3,512,4096]{2,1,0:T(8,128)} %get-tuple-element.471, f32[3,512]{1,0:T(4,128)S(1)} %get-tuple-element.472, pred[512,4096]{1,0:T(8,128)(4,1)S(1)} %broadcast_compare_fusion.4), kind=kLoop, calls=%fused_computation.4.clone.1 | loop fusion | flops 25164288 | bytes 27275264 | tf_op jit(solution)/shard_map/while/body/eval_jaxpr/reduce_sum | solution.py:169
  273.0 13.0 %fusion.116 = bf16[4,3,512,64]{2,3,1,0:T(8,128)(2,1)} fusion(bf16[4,3,512,64]{2,3,1,0:T(8,128)(2,1)} %get-tuple-element.500, s32[]{:T(128)S(6)} %copy.84, bf16[3,4096,64]{1,2,0:T(8,128)(2,1)} %get-tuple-element.520, f32[3,512,4096]{2,1,0:T(8,128)} %get-tuple-element.471, f32[3,512]{1,0:T(4,128)S(1)} %fusion.115, ...), kind=kOutput, calls=%fused_computation.9.clone.1 | convolution fusion | flops 836861952 | bytes 29044740 | tf_op jit(solution)/shard_map/while/body/eval_jaxpr/gqk,gkd->gqd/dot_general | solution.py:171
  288.7 12.2 %fusion.114 = (f32[3,512]{1,0:T(4,128)S(1)}, f32[3,512,4096]{2,1,0:T(8,128)}) fusion(pred[512,4096]{1,0:T(8,128)(4,1)S(1)} %broadcast_compare_fusion.4, bf16[3,4096,64]{1,2,0:T(8,128)(2,1)} %get-tuple-element.519, bf16[3,2048,64]{1,2,0:T(8,128)(2,1)S(1)} %get-tuple-element.518, s32[]{:T(128)S(6)} %select_n.67), kind=kOutput, calls=%fused_computation.3.clone.1 | convolution fusion | flops 824179200 | bytes 29038596 | tf_op jit(solution)/shard_map/while/body/eval_jaxpr/gqd,gkd->gqk/dot_general | solution.py:159
  300.9 11.8 %fusion.115 = f32[3,512]{1,0:T(4,128)S(1)} fusion(f32[3,512,4096]{2,1,0:T(8,128)} %get-tuple-element.471, f32[3,512]{1,0:T(4,128)S(1)} %get-tuple-element.472, pred[512,4096]{1,0:T(8,128)(4,1)S(1)} %broadcast_compare_fusion.4), kind=kLoop, calls=%fused_computation.4.clone.1 | loop fusion | flops 25164288 | bytes 27275264 | tf_op jit(solution)/shard_map/while/body/eval_jaxpr/reduce_sum | solution.py:169
  312.7 13.0 %fusion.116 = bf16[4,3,512,64]{2,3,1,0:T(8,128)(2,1)} fusion(bf16[4,3,512,64]{2,3,1,0:T(8,128)(2,1)} %get-tuple-element.500, s32[]{:T(128)S(6)} %copy.84, bf16[3,4096,64]{1,2,0:T(8,128)(2,1)} %get-tuple-element.520, f32[3,512,4096]{2,1,0:T(8,128)} %get-tuple-element.471, f32[3,512]{1,0:T(4,128)S(1)} %fusion.115, ...), kind=kOutput, calls=%fused_computation.9.clone.1 | convolution fusion | flops 836861952 | bytes 29044740 | tf_op jit(solution)/shard_map/while/body/eval_jaxpr/gqk,gkd->gqd/dot_general | solution.py:171
  330.0 10.9 %all-to-all-done.1 = bf16[4,512,1,192]{1,3,2,0:T(8,128)(2,1)S(1)} async-done(((bf16[4,512,1,192]{1,3,2,0:T(8,128)(2,1)}), bf16[4,512,1,192]{1,3,2,0:T(8,128)(2,1)S(1)}, u32[]{:S(2)}, u32[]{:S(2)}) %all-to-all-start.1) | async-done | bytes 786464 | tf_op jit(solution)/shard_map/all_to_all | solution.py:195
  351.8 7.7 fusion.70
  378.9 10.7 %fusion.54 = f32[3072,768]{1,0:T(8,128)} fusion(f32[512,768]{1,0:T(8,128)} %copy-done.9, f32[512,3072]{1,0:T(8,128)} %fusion.62, f32[3072]{0:T(1024)S(1)} %convert_element_type.104), kind=kOutput, calls=%fused_computation.116 | convolution fusion | flops 2432040960 | bytes 17313792 | tf_op jit(solution)/shard_map/ta,tb->ab/dot_general | solution.py:60
  414.7 362.3 %while.28 = (s32[]{:T(128)}, f32[2,3,4096,64]{2,3,1,0:T(8,128)}, bf16[4,3,512,64]{2,3,1,0:T(8,128)(2,1)}, s32[4]{0:T(128)S(1)}, s32[2048]{0:T(1024)S(1)}, /*inde...) while((s32[]{:T(128)}, f32[2,3,4096,64]{2,3,1,0:T(8,128)}, ...), condition=%wide.region_17.18_spmd.clone, body=%wide.region_15.17_spmd.clone.sunk | while | flops 4128602624 | bytes 284885344 | solution.py:275
  417.6 11.8 %fusion.126 = f32[3,512,4096]{2,1,0:T(8,128)} fusion(bf16[3,4096,64]{1,2,0:T(8,128)(2,1)} %get-tuple-element.562, bf16[3,2048,64]{1,2,0:T(8,128)(2,1)S(1)} %get-tuple-element.561, s32[]{:T(128)S(6)} %select_n.71), kind=kOutput, calls=%fused_computation.34.clone.1 | convolution fusion | flops 805306368 | bytes 26935300 | tf_op jit(solution)/shard_map/while/body/eval_jaxpr/gqd,gkd->gqk/dot_general | solution.py:159
  429.4 12.4 %fusion.127 = f32[1,3,4096,64]{2,3,1,0:T(8,128)} fusion(f32[3,512,4096]{2,1,0:T(8,128)} %fusion.126, f32[3,512]{1,0:T(4,128)S(1)} %dynamic-slice_bitcast_fusion.2, pred[512,4096]{1,0:T(8,128)(4,1)S(1)} %broadcast_compare_fusion.5, bf16[3,2048,64]{1,2,0:T(8,128)(2,1)} %get-tuple-element.564, s32[]{:T(128)S(6)} %select_n.71), kind=kOutput, calls=%fused_computation.23.clone.1 | convolution fusion | flops 830472192 | bytes 30611460 | tf_op jit(solution)/shard_map/while/body/eval_jaxpr/gqk,gqd->gkd/dot_general | solution.py:267
  441.8 18.3 %multiply_reduce_fusion.7 = (f32[3,512]{1,0:T(4,128)S(1)}, f32[3,512,4096]{2,1,0:T(8,128)}) fusion(f32[3,512,4096]{2,1,0:T(8,128)} %fusion.126, f32[3,512]{1,0:T(4,128)S(1)} %dynamic-slice_bitcast_fusion.2, pred[512,4096]{1,0:T(8,128)(4,1)S(1)} %broadcast_compare_fusion.5, bf16[3,4096,64]{1,2,0:T(8,128)(2,1)} %get-tuple-element.565, ...), kind=kOutput, calls=%fused_computation.17.clone.1 | convolution fusion | flops 836762112 | bytes 54210564 | tf_op jit(solution)/shard_map/while/body/eval_jaxpr/gqd,gkd->gqk/dot_general | solution.py:254
  460.1 22.0 %multiply_convert_fusion.5 = bf16[3,512,4096]{2,1,0:T(8,128)(2,1)} fusion(f32[3,512,4096]{2,1,0:T(8,128)} %get-tuple-element.484, f32[3,512,4096]{2,1,0:T(8,128)} %fusion.126, f32[3,512]{1,0:T(4,128)S(1)} %get-tuple-element.485, f32[3,512]{1,0:T(4,128)S(1)} %dynamic-slice_bitcast_fusion.2, pred[512,4096]{1,0:T(8,128)(4,1)S(1)} %broadcast_compare_fusion.5), kind=kLoop, calls=%fused_computation.16.clone.1 | loop fusion | flops 37748736 | bytes 65024000 | tf_op jit(solution)/shard_map/while/body/eval_jaxpr/convert_element_type | solution.py:258
  482.1 9.7 fusion.129
  491.8 7.6 fusion.128
  506.8 12.5 %fusion.126 = f32[3,512,4096]{2,1,0:T(8,128)} fusion(bf16[3,4096,64]{1,2,0:T(8,128)(2,1)} %get-tuple-element.562, bf16[3,2048,64]{1,2,0:T(8,128)(2,1)S(1)} %get-tuple-element.561, s32[]{:T(128)S(6)} %select_n.71), kind=kOutput, calls=%fused_computation.34.clone.1 | convolution fusion | flops 805306368 | bytes 26935300 | tf_op jit(solution)/shard_map/while/body/eval_jaxpr/gqd,gkd->gqk/dot_general | solution.py:159
  519.3 13.2 %fusion.127 = f32[1,3,4096,64]{2,3,1,0:T(8,128)} fusion(f32[3,512,4096]{2,1,0:T(8,128)} %fusion.126, f32[3,512]{1,0:T(4,128)S(1)} %dynamic-slice_bitcast_fusion.2, pred[512,4096]{1,0:T(8,128)(4,1)S(1)} %broadcast_compare_fusion.5, bf16[3,2048,64]{1,2,0:T(8,128)(2,1)} %get-tuple-element.564, s32[]{:T(128)S(6)} %select_n.71), kind=kOutput, calls=%fused_computation.23.clone.1 | convolution fusion | flops 830472192 | bytes 30611460 | tf_op jit(solution)/shard_map/while/body/eval_jaxpr/gqk,gqd->gkd/dot_general | solution.py:267
  532.5 19.1 %multiply_reduce_fusion.7 = (f32[3,512]{1,0:T(4,128)S(1)}, f32[3,512,4096]{2,1,0:T(8,128)}) fusion(f32[3,512,4096]{2,1,0:T(8,128)} %fusion.126, f32[3,512]{1,0:T(4,128)S(1)} %dynamic-slice_bitcast_fusion.2, pred[512,4096]{1,0:T(8,128)(4,1)S(1)} %broadcast_compare_fusion.5, bf16[3,4096,64]{1,2,0:T(8,128)(2,1)} %get-tuple-element.565, ...), kind=kOutput, calls=%fused_computation.17.clone.1 | convolution fusion | flops 836762112 | bytes 54210564 | tf_op jit(solution)/shard_map/while/body/eval_jaxpr/gqd,gkd->gqk/dot_general | solution.py:254
  551.6 22.3 %multiply_convert_fusion.5 = bf16[3,512,4096]{2,1,0:T(8,128)(2,1)} fusion(f32[3,512,4096]{2,1,0:T(8,128)} %get-tuple-element.484, f32[3,512,4096]{2,1,0:T(8,128)} %fusion.126, f32[3,512]{1,0:T(4,128)S(1)} %get-tuple-element.485, f32[3,512]{1,0:T(4,128)S(1)} %dynamic-slice_bitcast_fusion.2, pred[512,4096]{1,0:T(8,128)(4,1)S(1)} %broadcast_compare_fusion.5), kind=kLoop, calls=%fused_computation.16.clone.1 | loop fusion | flops 37748736 | bytes 65024000 | tf_op jit(solution)/shard_map/while/body/eval_jaxpr/convert_element_type | solution.py:258
  573.9 9.7 fusion.129
  598.1 11.7 %fusion.126 = f32[3,512,4096]{2,1,0:T(8,128)} fusion(bf16[3,4096,64]{1,2,0:T(8,128)(2,1)} %get-tuple-element.562, bf16[3,2048,64]{1,2,0:T(8,128)(2,1)S(1)} %get-tuple-element.561, s32[]{:T(128)S(6)} %select_n.71), kind=kOutput, calls=%fused_computation.34.clone.1 | convolution fusion | flops 805306368 | bytes 26935300 | tf_op jit(solution)/shard_map/while/body/eval_jaxpr/gqd,gkd->gqk/dot_general | solution.py:159
  609.8 12.4 %fusion.127 = f32[1,3,4096,64]{2,3,1,0:T(8,128)} fusion(f32[3,512,4096]{2,1,0:T(8,128)} %fusion.126, f32[3,512]{1,0:T(4,128)S(1)} %dynamic-slice_bitcast_fusion.2, pred[512,4096]{1,0:T(8,128)(4,1)S(1)} %broadcast_compare_fusion.5, bf16[3,2048,64]{1,2,0:T(8,128)(2,1)} %get-tuple-element.564, s32[]{:T(128)S(6)} %select_n.71), kind=kOutput, calls=%fused_computation.23.clone.1 | convolution fusion | flops 830472192 | bytes 30611460 | tf_op jit(solution)/shard_map/while/body/eval_jaxpr/gqk,gqd->gkd/dot_general | solution.py:267
  622.2 18.7 %multiply_reduce_fusion.7 = (f32[3,512]{1,0:T(4,128)S(1)}, f32[3,512,4096]{2,1,0:T(8,128)}) fusion(f32[3,512,4096]{2,1,0:T(8,128)} %fusion.126, f32[3,512]{1,0:T(4,128)S(1)} %dynamic-slice_bitcast_fusion.2, pred[512,4096]{1,0:T(8,128)(4,1)S(1)} %broadcast_compare_fusion.5, bf16[3,4096,64]{1,2,0:T(8,128)(2,1)} %get-tuple-element.565, ...), kind=kOutput, calls=%fused_computation.17.clone.1 | convolution fusion | flops 836762112 | bytes 54210564 | tf_op jit(solution)/shard_map/while/body/eval_jaxpr/gqd,gkd->gqk/dot_general | solution.py:254
  640.9 23.6 %multiply_convert_fusion.5 = bf16[3,512,4096]{2,1,0:T(8,128)(2,1)} fusion(f32[3,512,4096]{2,1,0:T(8,128)} %get-tuple-element.484, f32[3,512,4096]{2,1,0:T(8,128)} %fusion.126, f32[3,512]{1,0:T(4,128)S(1)} %get-tuple-element.485, f32[3,512]{1,0:T(4,128)S(1)} %dynamic-slice_bitcast_fusion.2, pred[512,4096]{1,0:T(8,128)(4,1)S(1)} %broadcast_compare_fusion.5), kind=kLoop, calls=%fused_computation.16.clone.1 | loop fusion | flops 37748736 | bytes 65024000 | tf_op jit(solution)/shard_map/while/body/eval_jaxpr/convert_element_type | solution.py:258
  664.5 10.1 %fusion.129 = bf16[4,3,512,64]{2,3,1,0:T(8,128)(2,1)} fusion(bf16[4,3,512,64]{2,3,1,0:T(8,128)(2,1)} %get-tuple-element.542, s32[]{:T(128)S(6)} %copy.93, bf16[3,512,4096]{2,1,0:T(8,128)(2,1)} %multiply_convert_fusion.5, bf16[3,4096,64]{1,2,0:T(8,128)(2,1)} %get-tuple-element.562), kind=kOutput, calls=%fused_computation.29.clone.1 | convolution fusion | flops 805404672 | bytes 14548996 | tf_op jit(solution)/shard_map/while/body/eval_jaxpr/gqk,gkd->gqd/dot_general | solution.py:260
  674.6 7.8 fusion.128
  689.8 11.9 %fusion.126 = f32[3,512,4096]{2,1,0:T(8,128)} fusion(bf16[3,4096,64]{1,2,0:T(8,128)(2,1)} %get-tuple-element.562, bf16[3,2048,64]{1,2,0:T(8,128)(2,1)S(1)} %get-tuple-element.561, s32[]{:T(128)S(6)} %select_n.71), kind=kOutput, calls=%fused_computation.34.clone.1 | convolution fusion | flops 805306368 | bytes 26935300 | tf_op jit(solution)/shard_map/while/body/eval_jaxpr/gqd,gkd->gqk/dot_general | solution.py:159
  701.7 12.8 %fusion.127 = f32[1,3,4096,64]{2,3,1,0:T(8,128)} fusion(f32[3,512,4096]{2,1,0:T(8,128)} %fusion.126, f32[3,512]{1,0:T(4,128)S(1)} %dynamic-slice_bitcast_fusion.2, pred[512,4096]{1,0:T(8,128)(4,1)S(1)} %broadcast_compare_fusion.5, bf16[3,2048,64]{1,2,0:T(8,128)(2,1)} %get-tuple-element.564, s32[]{:T(128)S(6)} %select_n.71), kind=kOutput, calls=%fused_computation.23.clone.1 | convolution fusion | flops 830472192 | bytes 30611460 | tf_op jit(solution)/shard_map/while/body/eval_jaxpr/gqk,gqd->gkd/dot_general | solution.py:267
  714.4 18.3 %multiply_reduce_fusion.7 = (f32[3,512]{1,0:T(4,128)S(1)}, f32[3,512,4096]{2,1,0:T(8,128)}) fusion(f32[3,512,4096]{2,1,0:T(8,128)} %fusion.126, f32[3,512]{1,0:T(4,128)S(1)} %dynamic-slice_bitcast_fusion.2, pred[512,4096]{1,0:T(8,128)(4,1)S(1)} %broadcast_compare_fusion.5, bf16[3,4096,64]{1,2,0:T(8,128)(2,1)} %get-tuple-element.565, ...), kind=kOutput, calls=%fused_computation.17.clone.1 | convolution fusion | flops 836762112 | bytes 54210564 | tf_op jit(solution)/shard_map/while/body/eval_jaxpr/gqd,gkd->gqk/dot_general | solution.py:254
  732.7 22.4 %multiply_convert_fusion.5 = bf16[3,512,4096]{2,1,0:T(8,128)(2,1)} fusion(f32[3,512,4096]{2,1,0:T(8,128)} %get-tuple-element.484, f32[3,512,4096]{2,1,0:T(8,128)} %fusion.126, f32[3,512]{1,0:T(4,128)S(1)} %get-tuple-element.485, f32[3,512]{1,0:T(4,128)S(1)} %dynamic-slice_bitcast_fusion.2, pred[512,4096]{1,0:T(8,128)(4,1)S(1)} %broadcast_compare_fusion.5), kind=kLoop, calls=%fused_computation.16.clone.1 | loop fusion | flops 37748736 | bytes 65024000 | tf_op jit(solution)/shard_map/while/body/eval_jaxpr/convert_element_type | solution.py:258
  755.1 9.8 fusion.129
  792.6 27.0 %collective-permute-done.2 = bf16[2,3,1024,64]{2,3,1,0:T(8,128)(2,1)} collective-permute-done((bf16[2,3,1024,64]{2,3,1,0:T(8,128)(2,1)}, bf16[2,3,1024,64]{2,3,1,0:T(8,128)(2,1)}, u32[]{:S(2)}, u32[]{:S(2)}) %collective-permute-start.2) | collective-permute-done | bytes 786464 | tf_op jit(solution)/shard_map/ppermute | solution.py:21
  825.0 31.0 %all_to_all.50 = bf16[4,512,3,1,192]{1,4,2,3,0:T(8,128)(2,1)S(1)} all-to-all(bf16[4,512,3,1,192]{1,4,2,3,0:T(8,128)(2,1)S(1)} %pad_maximum_fusion.1), channel_id=1, replica_groups=mesh['seq'=4,'shard'=8] {'seq'}, dimensions={0} | all-to-all | bytes 4718592 | tf_op jit(solution)/shard_map/all_to_all | solution.py:293
  862.0 8.0 copy.67
  871.5 42.2 %all-reduce.18 = (f32[768]{0:T(1024)S(1)}, f32[768]{0:T(1024)S(1)}, f32[768]{0:T(1024)S(1)}, f32[768]{0:T(1024)S(1)}, f32[768]{0:T(1024)S(1)}, /*index=5*/f32[30...) all-reduce(f32[768]{0:T(1024)S(1)} %get-tuple-element.261, ...), channel_id=3, replica_groups=mesh['seq'=4,'shard'=8] {'seq','shard'}, use_global_device_ids=true, to_apply=%region_20.21.clone | all-reduce | flops 9216 | bytes 73728
  924.6 65.8 %reduce-scatter.13.cloned.1.call-done = f32[24,2304]{1,0:T(8,128)} async-done(((f32[768,2304]{1,0:T(8,128)}), f32[24,2304]{1,0:T(8,128)}) %reduce-scatter.13.cloned.1.call-update) | async-done | bytes 221200
  (267 shorter events, 187.5 us)
Async XLA Ops:
  7.2 66.9 %all-gather.5.cloned.1.call-start = ((), (), s32[]{:S(2)}) async-start(), calls=%async_computation.8 | async-start | bytes 3649536 | tf_op jit(solution)/shard_map/all_gather | solution.py:112
  7.9 322.0 %all-gather.7.cloned.1.call-start = ((), (), s32[]{:S(2)}) async-start(), calls=%async_computation.9 | async-start | bytes 1216512 | tf_op jit(solution)/shard_map/all_gather | solution.py:115
  8.7 336.1 %all-gather.9.cloned.1.call-start = ((), (), s32[]{:S(2)}) async-start(), calls=%async_computation.10 | async-start | bytes 4866048 | tf_op jit(solution)/shard_map/all_gather | solution.py:119
  84.3 4.4 copy-start.26
  84.3 32.8 %all-to-all-start = ((bf16[512,3,4,192]{0,3,1,2:T(8,128)(2,1)}), bf16[512,3,4,192]{0,3,1,2:T(8,128)(2,1)S(1)}, u32[]{:S(2)}, u32[]{:S(2)}) async-start(bf16[512,3,4,192]{0,3,1,2:T(8,128)(2,1)} %copy.59), calls=%async_computation | async-start | bytes 4718592 | tf_op jit(solution)/shard_map/all_to_all | solution.py:186
  88.1 263.7 %all-gather.11.cloned.1.call-start = ((), (), s32[]{:S(2)}) async-start(), calls=%async_computation.11 | async-start | bytes 4866048 | tf_op jit(solution)/shard_map/all_gather | solution.py:121
  125.1 5.5 copy-start.3
  125.3 37.9 %collective-permute-start = (bf16[1024,2,192]{0,2,1:T(8,128)(2,1)S(1)}, bf16[1024,2,192]{0,2,1:T(8,128)(2,1)S(1)}, u32[]{:S(2)}, u32[]{:S(2)}) collective-permute-start(bf16[1024,2,192]{0,2,1:T(8,128)(2,1)S(1)} %get-tuple-element.344), channel_id=1, source_target_pairs={{0,1},{1,2},{2,3},{3,4},{4,5},{5,6},{6,7},{8,9},{9,10},{10,11},{11... | collective-permute-start | bytes 2359304 | tf_op jit(solution)/shard_map/ppermute | solution.py:21
  128.7 34.5 %collective-permute-start.1 = (bf16[1024,2,192]{0,2,1:T(8,128)(2,1)S(1)}, bf16[1024,2,192]{0,2,1:T(8,128)(2,1)S(1)}, u32[]{:S(2)}, u32[]{:S(2)}) collective-permute-start(bf16[1024,2,192]{0,2,1:T(8,128)(2,1)S(1)} %get-tuple-element.345), channel_id=1, source_target_pairs={{1,0},{2,1},{3,2},{4,3},{5,4},{6,5},{7,6},{9,8},{10,9},{11,10},{12... | collective-permute-start | bytes 2359304 | tf_op jit(solution)/shard_map/ppermute | solution.py:23
  165.5 164.3 %copy-start.25 = (bf16[768]{0:T(1024)(128)(2,1)S(1)}, bf16[768]{0:T(1024)(128)(2,1)}, u32[]{:S(2)}) copy-start(bf16[768]{0:T(1024)(128)(2,1)} %get-tuple-element.324) | copy-start | bytes 4612
  165.5 164.3 %copy-start.24 = (bf16[768]{0:T(1024)(128)(2,1)S(1)}, bf16[768]{0:T(1024)(128)(2,1)}, u32[]{:S(2)}) copy-start(bf16[768]{0:T(1024)(128)(2,1)} %get-tuple-element.323) | copy-start | bytes 4612
  165.5 164.3 %copy-start.23 = (bf16[768]{0:T(1024)(128)(2,1)S(1)}, bf16[768]{0:T(1024)(128)(2,1)}, u32[]{:S(2)}) copy-start(bf16[768]{0:T(1024)(128)(2,1)} %get-tuple-element.327) | copy-start | bytes 4612
  165.5 164.3 %copy-start.22 = (bf16[768]{0:T(1024)(128)(2,1)S(1)}, bf16[768]{0:T(1024)(128)(2,1)}, u32[]{:S(2)}) copy-start(bf16[768]{0:T(1024)(128)(2,1)} %get-tuple-element.321) | copy-start | bytes 4612
  165.5 164.3 %copy-start.21 = (bf16[768]{0:T(1024)(128)(2,1)S(1)}, bf16[768]{0:T(1024)(128)(2,1)}, u32[]{:S(2)}) copy-start(bf16[768]{0:T(1024)(128)(2,1)} %get-tuple-element.322) | copy-start | bytes 4612
  165.6 164.3 %copy-start.20 = (bf16[768]{0:T(1024)(128)(2,1)S(1)}, bf16[768]{0:T(1024)(128)(2,1)}, u32[]{:S(2)}) copy-start(bf16[768]{0:T(1024)(128)(2,1)} %get-tuple-element.326) | copy-start | bytes 4612
  165.6 164.3 %copy-start.17 = (bf16[3072]{0:T(1024)(128)(2,1)S(1)}, bf16[3072]{0:T(1024)(128)(2,1)}, u32[]{:S(2)}) copy-start(bf16[3072]{0:T(1024)(128)(2,1)} %get-tuple-element.325) | copy-start | bytes 18436
  325.7 15.1 %all-to-all-start.1 = ((bf16[4,512,1,192]{1,3,2,0:T(8,128)(2,1)}), bf16[4,512,1,192]{1,3,2,0:T(8,128)(2,1)S(1)}, u32[]{:S(2)}, u32[]{:S(2)}) async-start(bf16[4,512,1,192]{1,3,2,0:T(8,128)(2,1)} %bitcast.14), calls=%async_computation.1 | async-start | bytes 1572864 | tf_op jit(solution)/shard_map/all_to_all | solution.py:195
  329.3 595.3 %reduce-scatter.7.cloned.1.call-start = ((), (), s32[]{:S(2)}) async-start(), calls=%async_computation.12 | async-start | bytes 2433024 | tf_op jit(solution)/shard_map/reduce_scatter | solution.py:328
  351.8 8.1 copy-start.8
  351.8 11.5 %copy-start.28 = (f32[512,3072]{1,0:T(8,128)S(1)}, f32[512,3072]{1,0:T(8,128)}, u32[]{:S(2)}) copy-start(f32[512,3072]{1,0:T(8,128)} %fusion.62) | copy-start | bytes 18874372
  359.9 3.5 copy-start.27
  361.2 9.3 slice-start.3
  363.4 7.1 copy-start.9
  363.4 7.1 slice-start.4
  370.5 3.6 copy-start.29
  378.7 545.9 %reduce-scatter.11.cloned.1.call-start = ((), (), s32[]{:S(2)}) async-start(), calls=%async_computation.14 | async-start | bytes 9732096 | tf_op jit(solution)/shard_map/reduce_scatter | solution.py:334
  395.5 15.9 %all-to-all-start.2 = ((bf16[1,512,4,192]{1,3,0,2:T(8,128)(2,1)}), bf16[1,512,4,192]{1,3,0,2:T(8,128)(2,1)}, u32[]{:S(2)}, u32[]{:S(2)}) async-start(bf16[1,512,4,192]{1,3,0,2:T(8,128)(2,1)} %bitcast.132), calls=%async_computation.2 | async-start | bytes 1572864 | tf_op jit(solution)/shard_map/all_to_all | solution.py:237
  399.7 524.9 %reduce-scatter.9.cloned.1.call-start = ((), (), s32[]{:S(2)}) async-start(), calls=%async_computation.13 | async-start | bytes 9732096 | tf_op jit(solution)/shard_map/reduce_scatter | solution.py:332
  407.2 583.2 %reduce-scatter.13.cloned.1.call-start = ((), (), s32[]{:S(2)}) async-start(), calls=%async_computation.15 | async-start | bytes 7299072
  482.1 17.3 %slice-start = ((s8[6291456]{0:T(1024)(128)(4,1)}), s8[2097152]{0:T(1024)(128)(4,1)S(1)}, s32[]{:S(2)}) async-start(s8[6291456]{0:T(1024)(128)(4,1)} %bitcast.121), calls=%async_computation.16 | async-start | bytes 4194304 | tf_op jit(solution)/shard_map/while
  491.8 7.6 slice-start.1
  491.8 7.6 copy-start.2
  501.5 2.6 copy-start
  573.9 16.8 %slice-start = ((s8[6291456]{0:T(1024)(128)(4,1)}), s8[2097152]{0:T(1024)(128)(4,1)S(1)}, s32[]{:S(2)}) async-start(s8[6291456]{0:T(1024)(128)(4,1)} %bitcast.121), calls=%async_computation.16 | async-start | bytes 4194304 | tf_op jit(solution)/shard_map/while
  583.6 7.1 slice-start.1
  583.6 7.1 copy-start.2
  592.8 2.6 copy-start
  664.5 17.9 %slice-start = ((s8[6291456]{0:T(1024)(128)(4,1)}), s8[2097152]{0:T(1024)(128)(4,1)S(1)}, s32[]{:S(2)}) async-start(s8[6291456]{0:T(1024)(128)(4,1)} %bitcast.121), calls=%async_computation.16 | async-start | bytes 4194304 | tf_op jit(solution)/shard_map/while
  674.6 7.9 slice-start.1
  674.6 7.9 copy-start.2
  684.5 2.6 copy-start
  755.1 16.9 %slice-start = ((s8[6291456]{0:T(1024)(128)(4,1)}), s8[2097152]{0:T(1024)(128)(4,1)S(1)}, s32[]{:S(2)}) async-start(s8[6291456]{0:T(1024)(128)(4,1)} %bitcast.121), calls=%async_computation.16 | async-start | bytes 4194304 | tf_op jit(solution)/shard_map/while
  764.9 7.1 slice-start.1
  764.9 7.1 copy-start.2
  774.0 2.6 copy-start
  777.1 11.0 %copy-start.1 = (f32[2,3,4096,64]{2,3,1,0:T(8,128)S(1)}, f32[2,3,4096,64]{2,3,1,0:T(8,128)}, u32[]{:S(2)}) copy-start(f32[2,3,4096,64]{2,3,1,0:T(8,128)} %get-tuple-element.148) | copy-start | bytes 18874372
  781.7 37.9 %collective-permute-start.2 = (bf16[2,3,1024,64]{2,3,1,0:T(8,128)(2,1)}, bf16[2,3,1024,64]{2,3,1,0:T(8,128)(2,1)}, u32[]{:S(2)}, u32[]{:S(2)}) collective-permute-start(bf16[2,3,1024,64]{2,3,1,0:T(8,128)(2,1)} %get-tuple-element.336), channel_id=1, source_target_pairs={{0,1},{1,2},{2,3},{3,4},{4,5},{5,6},{6,7},{8,9},{9,10},{10,11},{11... | collective-permute-start | bytes 2359304 | tf_op jit(solution)/shard_map/ppermute | solution.py:21
  786.6 33.0 %collective-permute-start.3 = (bf16[2,3,1024,64]{2,3,1,0:T(8,128)(2,1)}, bf16[2,3,1024,64]{2,3,1,0:T(8,128)(2,1)}, u32[]{:S(2)}, u32[]{:S(2)}) collective-permute-start(bf16[2,3,1024,64]{2,3,1,0:T(8,128)(2,1)} %get-tuple-element.337), channel_id=1, source_target_pairs={{1,0},{2,1},{3,2},{4,3},{5,4},{6,5},{7,6},{9,8},{10,9},{11,10},{12... | collective-permute-start | bytes 2359304 | tf_op jit(solution)/shard_map/ppermute | solution.py:23
  (14 other events, 15.1 us)
Sparse Core Ops, SparseCore 0:
  11.0 63.0 all-gather.4
  77.1 53.0 all-gather.6
  133.2 68.0 all-gather.8
  204.1 62.4 all-gather.10
  378.8 98.7 reduce-scatter.6
  484.9 134.3 reduce-scatter.10
  625.8 134.8 reduce-scatter.8
  870.2 120.1 reduce-scatter.12
